TPU v7x, 512 devices: a whole 4x8x8 slice. The times are simulated.
512 devices in a mesh: tile: 32 (over y, x), tm: 16 (over z, core).
Axes of the slice: x: 4, y: 8, z: 8, core: 2. Of those that a mesh axis runs over, the one named last changes fastest.
Arguments:
- movie: bfloat16 [256, 256, 4096], P('tm', None, 'tile'), may hold values from -6 to 6
- omega: bfloat16 [2, 32, 32, 256], P(None, 'tile', None, 'tm'), may hold values from -0.375 to 0.375
- time_taps: bfloat16 [17], replicated, may hold values from 0.019897461 to 0.099609375
- space_taps: bfloat16 [17], replicated, may hold values from 0.099609375 to 0.29882812
Outputs:
- basis: float32 [32, 256, 4096], P(None, 'tm', 'tile')
- coefficients: float32 [2, 32, 32, 256], P(None, 'tile', None, 'tm')
All inputs are finite; a program needn't handle non-finite values.
Results may differ from a plain program's by a relative error of at most 0.024.
Values may be sent and summed in bfloat16 or wider, within the bound.
A program may use at most 64 MiB of HBM per device.

v0:
```python
import math

import jax
import jax.numpy as jnp
from jax import lax
from jax.sharding import PartitionSpec as P

H = 128
TY = 2


def with_halo(block, sides, width):
    for axis, dim in sides:
        count = lax.axis_size(axis)
        forward = [(i, i + 1) for i in range(count - 1)]
        backward = [(target, source) for source, target in forward]
        low = lax.ppermute(
            lax.slice_in_dim(block, block.shape[dim] - width, None, axis=dim), axis, forward
        )
        high = lax.ppermute(lax.slice_in_dim(block, 0, width, axis=dim), axis, backward)
        block = jnp.concatenate([low, block, high], axis=dim)
    return block


def band(tap_row, out_count, in_count, offset_by):
    row_ids = lax.broadcasted_iota(jnp.int32, (out_count, in_count), 0)
    col_ids = lax.broadcasted_iota(jnp.int32, (out_count, in_count), 1)
    offsets = col_ids - row_ids + offset_by
    picks = jnp.arange(tap_row.shape[0], dtype=jnp.int32)
    hits = (offsets[:, :, None] == picks).astype(jnp.float32)
    return jnp.sum(hits * tap_row.astype(jnp.float32), axis=2).astype(jnp.bfloat16)


def orthonormal(matrix):
    gram_block = jnp.dot(matrix, matrix.T, precision=lax.Precision.HIGHEST)
    factor_low = jnp.linalg.cholesky(gram_block)
    return jax.scipy.linalg.solve_triangular(factor_low, matrix, lower=True)


def local(movie, omega, time_taps, space_taps):
    frames, image_rows, tile_cols = movie.shape
    radius = (time_taps.shape[0] - 1) // 2
    tile_rows = H
    stack = TY
    pixels = tile_rows * tile_cols
    rank_count = omega.shape[2]
    row_share = image_rows // lax.axis_size("tm")
    time_band = band(time_taps, frames, frames + 2 * radius, 0)
    padded = with_halo(movie, (("tm", 0),), radius)
    flat_rows = padded.reshape(frames + 2 * radius, image_rows * tile_cols)
    low_time = jnp.dot(time_band, flat_rows, preferred_element_type=jnp.float32)
    centre = flat_rows[radius : radius + frames].astype(jnp.float32)
    temporal = (centre - low_time).astype(jnp.bfloat16).reshape(frames, image_rows, tile_cols)
    temporal = with_halo(temporal, (("tile", 2),), radius)
    across = band(space_taps, tile_cols, tile_cols + 2 * radius, 0).T
    smooth_x = jnp.dot(temporal, across, preferred_element_type=jnp.float32).astype(jnp.bfloat16)
    down_band = band(space_taps, image_rows, image_rows, radius)
    lowpass = jnp.einsum("ab,fbw->faw", down_band, smooth_x, preferred_element_type=jnp.float32)
    centre_z = temporal[:, :, radius : radius + tile_cols].astype(jnp.float32)
    filtered = (centre_z - lowpass).astype(jnp.bfloat16).reshape(frames, stack, pixels)
    row_start = lax.axis_index("tm") * row_share

    def to_image(tiled):
        shaped = tiled.reshape(stack, rank_count, tile_rows, tile_cols)
        return jnp.transpose(shaped, (1, 0, 2, 3)).reshape(rank_count, image_rows, tile_cols)

    def subspace(partial_value):
        summed = lax.psum(partial_value.astype(jnp.bfloat16), "tm").astype(jnp.float32)
        basis_all = jax.vmap(orthonormal)(summed)
        own_rows = lax.dynamic_slice_in_dim(to_image(basis_all), row_start, row_share, 1)
        return (basis_all.astype(jnp.bfloat16), own_rows)

    omega_local = omega[:, 0]
    sketch = jnp.einsum("tkf,ftp->tkp", omega_local, filtered, preferred_element_type=jnp.float32)
    first_basis, unused_rows = subspace(sketch)
    loadings = jnp.einsum(
        "ftp,tkp->ftk", filtered, first_basis, preferred_element_type=jnp.float32
    ).astype(jnp.bfloat16)
    refined = jnp.einsum("ftk,ftp->tkp", loadings, filtered, preferred_element_type=jnp.float32)
    final_basis, final_rows = subspace(refined)
    coefficients = jnp.einsum(
        "tkp,ftp->tkf", final_basis, filtered, preferred_element_type=jnp.float32
    )
    return (final_rows * math.sqrt(pixels), coefficients[:, None])


def solution(mesh):
    in_specs = (P("tm", None, "tile"), P(None, "tile", None, "tm"), P(), P())
    out_specs = (P(None, "tm", "tile"), P(None, "tile", None, "tm"))
    return jax.shard_map(local, mesh=mesh, in_specs=in_specs, out_specs=out_specs, check_vma=False)
```

profile of v0, /device:TPU:1, one launch (start us, length us, event | category | flops | bytes accessed | tf_op | source)
XLA Modules:
  0.0 342.5 jit_solution(9455576074152000294)
XLA Ops:
  7.2 0.0 copy-start
  7.2 0.0 copy-start.3
  7.2 0.0 all-reduce.3.cloned.1.call-start
  7.2 1.4 fusion.46
  8.6 0.0 copy-start.4
  8.6 0.0 copy-start.5
  8.6 5.4 %collective-permute-start = (bf16[8,256,128]{2,1,0:T(8,128)(2,1)S(1)}, bf16[8,256,128]{2,1,0:T(8,128)(2,1)S(1)}, u32[]{:S(2)}, u32[]{:S(2)}) collective-permute-start(bf16[8,256,128]{2,1,0:T(8,128)(2,1)S(1)} %get-tuple-element.14), channel_id=1, source_target_pairs={{0,1},{1,2},{2,3},{3,4},{4,5},{5,6},{6,7},{7,8},{8,9},{9,10},{10,1... | collective-permute-start | bytes 1572872 | tf_op jit(solution)/shard_map/ppermute | solution.py:17
  14.0 4.7 %collective-permute-start.1 = (bf16[8,256,128]{2,1,0:T(8,128)(2,1)S(1)}, bf16[8,256,128]{2,1,0:T(8,128)(2,1)S(1)}, u32[]{:S(2)}, u32[]{:S(2)}) collective-permute-start(bf16[8,256,128]{2,1,0:T(8,128)(2,1)S(1)} %get-tuple-element.15), channel_id=1, source_target_pairs={{1,0},{2,1},{3,2},{4,3},{5,4},{6,5},{7,6},{8,7},{9,8},{10,9},{11,1... | collective-permute-start | bytes 1572872 | tf_op jit(solution)/shard_map/ppermute | solution.py:20
  18.8 0.0 copy-done.3
  18.8 0.2 convert.1
  19.0 0.0 copy-done.4
  19.0 0.0 copy-done.5
  19.0 0.1 select_reduce_fusion.2
  19.2 0.5 select_reduce_fusion
  19.7 0.5 collective-permute-done
  20.1 4.4 %collective-permute-done.1 = bf16[8,256,128]{2,1,0:T(8,128)(2,1)S(1)} collective-permute-done((bf16[8,256,128]{2,1,0:T(8,128)(2,1)S(1)}, bf16[8,256,128]{2,1,0:T(8,128)(2,1)S(1)}, u32[]{:S(2)}, u32[]{:S(2)}) %collective-permute-start.1) | collective-permute-done | bytes 524320 | tf_op jit(solution)/shard_map/ppermute | solution.py:20
  24.5 0.2 pad_maximum_fusion
  24.8 2.3 fusion.10
  27.1 0.2 copy.59
  27.3 0.5 copy.38
  27.8 3.1 collective-permute-start.2
  31.0 1.3 collective-permute-start.3
  32.3 0.2 select_reduce_fusion.1
  32.4 0.0 collective-permute-done.2
  32.5 3.5 %collective-permute-done.3 = bf16[16,256,8]{1,2,0:T(8,128)(2,1)S(1)} collective-permute-done((bf16[16,256,8]{1,2,0:T(8,128)(2,1)S(1)}, bf16[16,256,8]{1,2,0:T(8,128)(2,1)S(1)}, u32[]{:S(2)}, u32[]{:S(2)}) %collective-permute-start.3) | collective-permute-done | bytes 65568 | tf_op jit(solution)/shard_map/ppermute | solution.py:20
  36.0 1.5 fusion.7
  37.5 0.7 copy.43
  38.2 0.3 reshape.57
  38.5 0.0 copy-done
  38.5 2.6 fusion.1
  41.1 0.0 all-reduce.3.cloned.1.call-update
  41.2 0.0 all-reduce.5.cloned.1.call-start
  41.2 127.3 %all-reduce.3.cloned.1.call-done = bf16[2,32,16384]{2,1,0:T(8,128)(2,1)} async-done(((bf16[2,32,16384]{2,1,0:T(8,128)(2,1)}), bf16[2,32,16384]{2,1,0:T(8,128)(2,1)}) %all-reduce.3.cloned.1.call-update) | async-done | bytes 2097168 | tf_op jit(solution)/shard_map/psum | solution.py:68
  168.6 0.0 copy-start.2
  168.6 3.0 fusion.47
  171.6 0.1 copy.45
  171.7 6.0 %custom-call.8 = f32[2,32,32]{2,1,0:T(8,128)S(1)} custom-call(f32[2,32,32]{2,1,0:T(8,128)S(1)} %fusion.40), custom_call_target="Cholesky" | custom-call | tf_op jit(solution)/shard_map/vmap(jit(cholesky))/cholesky | solution.py:36
  177.8 0.1 compare_reduce_fusion.1
  177.9 0.1 select_bitcast_fusion.1
  178.0 4.9 %custom-call.9 = f32[2,1,32,32]{2,3,1,0:T(8,128)S(1)} custom-call(f32[2,1,32,32]{3,2,1,0:T(8,128)S(1)} %select_bitcast_fusion.1), custom_call_target="InvertDiagBlocksLowerTriangular" | custom-call | tf_op jit(solution)/shard_map/vmap(jit(_solve_triangular))/triangular_solve | solution.py:37
  182.9 0.0 copy-done.2
  182.9 4.8 %convolution_convert_fusion.1 = bf16[2,32,16384]{2,1,0:T(8,128)(2,1)} fusion(bf16[2,32,16384]{2,1,0:T(8,128)(2,1)S(1)} %copy-done.2, f32[2,1,32,32]{2,3,1,0:T(8,128)S(1)} %custom-call.9), kind=kOutput, calls=%fused_computation.3 | convolution fusion | flops 404750336 | bytes 4202496 | tf_op jit(solution)/shard_map/vmap(jit(_solve_triangular))/triangular_solve | solution.py:37
  187.7 5.3 %convolution_convert_fusion = bf16[2,32,16384]{2,1,0:T(8,128)(2,1)} fusion(bf16[2,32,16384]{2,1,0:T(8,128)(2,1)} %convolution_convert_fusion.1, bf16[16,2,16384]{2,1,0:T(2,128)(2,1)S(1)} %reshape.57), kind=kOutput, calls=%fused_computation.2 | convolution fusion | flops 68158464 | bytes 5242880 | tf_op jit(solution)/shard_map/ftk,ftp->tkp/dot_general | solution.py:79
  192.9 0.0 all-reduce.5.cloned.1.call-update
  193.0 120.7 %all-reduce.5.cloned.1.call-done = bf16[2,32,16384]{2,1,0:T(8,128)(2,1)} async-done(((bf16[2,32,16384]{2,1,0:T(8,128)(2,1)}), bf16[2,32,16384]{2,1,0:T(8,128)(2,1)}) %all-reduce.5.cloned.1.call-update) | async-done | bytes 2097168 | tf_op jit(solution)/shard_map/psum | solution.py:68
  313.7 0.0 copy-start.1
  313.7 3.0 fusion.48
  316.7 0.1 copy.49
  316.8 5.9 %custom-call.10 = f32[2,32,32]{2,1,0:T(8,128)S(1)} custom-call(f32[2,32,32]{2,1,0:T(8,128)S(1)} %fusion.38), custom_call_target="Cholesky" | custom-call | tf_op jit(solution)/shard_map/vmap(jit(cholesky))/cholesky | solution.py:36
  322.7 0.1 compare_reduce_fusion
  322.9 0.1 select_bitcast_fusion
  322.9 4.9 %custom-call.11 = f32[2,1,32,32]{2,3,1,0:T(8,128)S(1)} custom-call(f32[2,1,32,32]{3,2,1,0:T(8,128)S(1)} %select_bitcast_fusion), custom_call_target="InvertDiagBlocksLowerTriangular" | custom-call | tf_op jit(solution)/shard_map/vmap(jit(_solve_triangular))/triangular_solve | solution.py:37
  327.9 0.0 copy-done.1
  327.9 3.9 %fusion.2 = f32[2,32,16384]{2,1,0:T(8,128)S(1)} fusion(bf16[2,32,16384]{2,1,0:T(8,128)(2,1)S(1)} %copy-done.1, f32[2,1,32,32]{2,3,1,0:T(8,128)S(1)} %custom-call.11), kind=kOutput, calls=%fused_computation.9 | convolution fusion | flops 403701760 | bytes 6299648 | tf_op jit(solution)/shard_map/vmap(jit(_solve_triangular))/triangular_solve | solution.py:37
  331.7 1.5 fusion.23
  333.2 0.7 copy.60
  333.9 0.5 bitcast_bitcast_fusion
  334.4 0.5 copy.51
  334.9 0.7 dynamic-slice_multiply_fusion
  (12 shorter events, 0.2 us)
Async XLA Ops:
  7.2 31.3 %copy-start = (bf16[2,1,32,16]{2,3,1,0:T(8,128)(2,1)S(1)}, bf16[2,1,32,16]{2,3,1,0:T(8,128)(2,1)}, u32[]{:S(2)}) copy-start(bf16[2,1,32,16]{2,3,1,0:T(8,128)(2,1)} %param.8) | copy-start | bytes 6148
  7.2 11.6 %copy-start.3 = (bf16[16,256,128]{2,1,0:T(8,128)(2,1)S(1)}, bf16[16,256,128]{2,1,0:T(8,128)(2,1)}, u32[]{:S(2)}) copy-start(bf16[16,256,128]{2,1,0:T(8,128)(2,1)} %param.7) | copy-start | bytes 3145732
  7.2 161.4 %all-reduce.3.cloned.1.call-start = ((), (), s32[]{:S(2)}) async-start(), calls=%async_computation | async-start | bytes 4194304 | tf_op jit(solution)/shard_map/psum | solution.py:68
  8.6 10.4 %copy-start.4 = (bf16[17]{0:T(256)(128)(2,1)S(1)}, bf16[17]{0:T(256)(128)(2,1)}, u32[]{:S(2)}) copy-start(bf16[17]{0:T(256)(128)(2,1)} %param.9) | copy-start | bytes 106
  8.6 10.4 %copy-start.5 = (bf16[17]{0:T(256)(128)(2,1)S(1)}, bf16[17]{0:T(256)(128)(2,1)}, u32[]{:S(2)}) copy-start(bf16[17]{0:T(256)(128)(2,1)} %param.10) | copy-start | bytes 106
  8.6 11.5 %collective-permute-start = (bf16[8,256,128]{2,1,0:T(8,128)(2,1)S(1)}, bf16[8,256,128]{2,1,0:T(8,128)(2,1)S(1)}, u32[]{:S(2)}, u32[]{:S(2)}) collective-permute-start(bf16[8,256,128]{2,1,0:T(8,128)(2,1)S(1)} %get-tuple-element.14), channel_id=1, source_target_pairs={{0,1},{1,2},{2,3},{3,4},{4,5},{5,6},{6,7},{7,8},{8,9},{9,10},{10,1... | collective-permute-start | bytes 1572872 | tf_op jit(solution)/shard_map/ppermute | solution.py:17
  14.0 10.5 %collective-permute-start.1 = (bf16[8,256,128]{2,1,0:T(8,128)(2,1)S(1)}, bf16[8,256,128]{2,1,0:T(8,128)(2,1)S(1)}, u32[]{:S(2)}, u32[]{:S(2)}) collective-permute-start(bf16[8,256,128]{2,1,0:T(8,128)(2,1)S(1)} %get-tuple-element.15), channel_id=1, source_target_pairs={{1,0},{2,1},{3,2},{4,3},{5,4},{6,5},{7,6},{8,7},{9,8},{10,9},{11,1... | collective-permute-start | bytes 1572872 | tf_op jit(solution)/shard_map/ppermute | solution.py:20
  27.8 4.6 %collective-permute-start.2 = (bf16[16,256,8]{1,2,0:T(8,128)(2,1)S(1)}, bf16[16,256,8]{1,2,0:T(8,128)(2,1)S(1)}, u32[]{:S(2)}, u32[]{:S(2)}) collective-permute-start(bf16[16,256,8]{1,2,0:T(8,128)(2,1)S(1)} %get-tuple-element.12), channel_id=1, source_target_pairs={{0,16},{16,32},{32,48},{48,64},{64,80},{80,96},{96,112},{112,128},... | collective-permute-start | bytes 196616 | tf_op jit(solution)/shard_map/ppermute | solution.py:17
  31.0 5.0 %collective-permute-start.3 = (bf16[16,256,8]{1,2,0:T(8,128)(2,1)S(1)}, bf16[16,256,8]{1,2,0:T(8,128)(2,1)S(1)}, u32[]{:S(2)}, u32[]{:S(2)}) collective-permute-start(bf16[16,256,8]{1,2,0:T(8,128)(2,1)S(1)} %get-tuple-element.13), channel_id=1, source_target_pairs={{16,0},{32,16},{48,32},{64,48},{80,64},{96,80},{112,96},{128,112},... | collective-permute-start | bytes 196616 | tf_op jit(solution)/shard_map/ppermute | solution.py:20
  41.2 272.5 %all-reduce.5.cloned.1.call-start = ((), (), s32[]{:S(2)}) async-start(), calls=%async_computation.1 | async-start | bytes 4194304 | tf_op jit(solution)/shard_map/psum | solution.py:68
  168.6 14.3 %copy-start.2 = (bf16[2,32,16384]{2,1,0:T(8,128)(2,1)S(1)}, bf16[2,32,16384]{2,1,0:T(8,128)(2,1)}, u32[]{:S(2)}) copy-start(bf16[2,32,16384]{2,1,0:T(8,128)(2,1)} %all-reduce.3.cloned.1.call-done) | copy-start | bytes 6291460
  313.7 14.2 %copy-start.1 = (bf16[2,32,16384]{2,1,0:T(8,128)(2,1)S(1)}, bf16[2,32,16384]{2,1,0:T(8,128)(2,1)}, u32[]{:S(2)}) copy-start(bf16[2,32,16384]{2,1,0:T(8,128)(2,1)} %all-reduce.5.cloned.1.call-done) | copy-start | bytes 6291460
Sparse Core Ops, SparseCore 0:
  41.3 127.2 all-reduce.2
  193.1 120.5 all-reduce.4
where the time goes:
time: 343 us; the launch traced here: 342 us
  waiting for transfers between devices  256 us (75%)
  matrix products  27.9 us (8%)
  other arithmetic  24.2 us (7%)
  starting transfers between devices  14.6 us (4%)
  between operations  14.3 us (4%)
  local copies, waits for them, and re-layouts  4.95 us (1%)
    psum x2, waiting for transfers between devices, subspace(): lax.psum(partial_value.astype(jnp.bfloat16), 'tm').astype(jnp.float32)  248 us
    another operation x7, other arithmetic, orthonormal(): factor_low = jnp.linalg.cholesky(gram_block)  12.2 us
    another operation x5, other arithmetic, orthonormal(): return jax.scipy.linalg.solve_triangular(factor_low, matrix, lower=True)  9.99 us
    another operation x2, matrix products, orthonormal(): return jax.scipy.linalg.solve_triangular(factor_low, matrix, lower=True)  8.65 us
    ppermute x2, starting transfers between devices, with_halo(): lax.ppermute(lax.slice_in_dim(block, block.shape[dim] - width, None, axis...  8.51 us
    ppermute x2, waiting for transfers between devices, with_halo(): lax.ppermute(lax.slice_in_dim(block, 0, width, axis=dim), axis, backward)  7.9 us
  transfers between devices with their start and end apart: 6, of which 5 were waited for; matrix products, arithmetic and copies ran while one was open for 0% of the time, Pallas kernels for 0%

commit v1 on v0

v1 whole, which is shorter than its diff:
```python
import functools
import math

import jax
import jax.numpy as jnp
from jax import lax
from jax.experimental import pallas as pl
from jax.experimental.pallas import tpu as pltpu
from jax.sharding import PartitionSpec as P

MESH = pl.DeviceIdType.MESH
F32 = jnp.float32
BF16 = jnp.bfloat16
HIGHEST = lax.Precision.HIGHEST

N_TM = 16
HALF = 8
FR = 16
FRAMES = 256
ROWS = 256
SHARE = 16
W = 128
K = 32
RAD = 8
PIX = SHARE * W


def mm(a, b, **kw):
    return jnp.dot(a, b, preferred_element_type=F32, **kw)


def mm_nt(a, b, **kw):
    return lax.dot_general(a, b, (((1,), (1,)), ((), ())), preferred_element_type=F32, **kw)


def mm_tn(a, b, **kw):
    return lax.dot_general(a, b, (((0,), (0,)), ((), ())), preferred_element_type=F32, **kw)


def pieces(x, count):
    out = []
    for _ in range(count - 1):
        part = x.astype(BF16)
        out.append(part)
        x = x - part.astype(F32)
    out.append(x.astype(BF16))
    return out


def stacked(x, count, axis=0):
    return jnp.concatenate(pieces(x, count), axis=axis)


def fold(x, count):
    total = x[:K]
    for i in range(1, count):
        total = total + x[i * K : (i + 1) * K]
    return total


def fold_lanes(x, count):
    total = x[:, :K]
    for i in range(1, count):
        total = total + x[:, i * K : (i + 1) * K]
    return total


def iota(shape, dim):
    return lax.broadcasted_iota(jnp.int32, shape, dim)


def from_taps(taps, index):
    out = jnp.zeros(index.shape, F32)
    for k in range(2 * RAD + 1):
        out = jnp.where(index == k, taps[:, k : k + 1], out)
    return out


def gram(x3):
    return fold_lanes(fold(mm_nt(x3, x3), 3), 3)


def inverse_factor(g):
    lane = iota((K, 128), 1)
    row = iota((K, 128), 0)
    aug = jnp.concatenate([g, jnp.where(iota((K, K), 0) == iota((K, K), 1), 1.0, 0.0), jnp.zeros((K, 64), F32)], axis=1)
    pivots = jnp.zeros((K, 128), F32)
    for j in range(K):
        line = aug[j : j + 1, :]
        pivot = line[:, j : j + 1]
        column = jnp.where(row > j, aug[:, j : j + 1], 0.0)
        pivots = jnp.where(row == j, pivot, pivots)
        aug = aug - column * (line / pivot)
    return (aug * lax.rsqrt(pivots))[:, K : 2 * K]


def kernel(
    n_tile,
    movie_hbm, omega_ref, time_ref, space_ref,
    basis_ref, coef_ref,
    movie, far, packed, edge, turn, out_buf, seen, om_all,
    b_slots, g_slots, b_mine, g_mine, f_mine, f_slots, y_buf, r_buf,
    load_sem, halo_s, halo_r, s_s, s_r, om_s, om_r, b_s, b_r, g_s, g_r, f_s, f_r,
):
    tile = lax.axis_index("tile")
    me = lax.axis_index("tm")
    half = me // HALF
    place = me - half * HALF
    left = lax.rem(tile + n_tile - 1, n_tile)
    right = lax.rem(tile + 1, n_tile)

    load = pltpu.make_async_copy(movie_hbm, movie, load_sem)
    load.start()
    barrier = pltpu.get_barrier_semaphore()
    for k in (8, 7, 9, 6, 10, 5, 11, 4, 12, 3, 13, 2, 14, 1, 15):
        pl.semaphore_signal(barrier, inc=1, device_id=(tile, lax.rem(me + k, N_TM)), device_id_type=MESH)
    pl.semaphore_signal(barrier, inc=1, device_id=(left, me), device_id_type=MESH)
    pl.semaphore_signal(barrier, inc=1, device_id=(right, me), device_id_type=MESH)

    space = space_ref[...].astype(F32)
    load.wait()

    lane = iota((W, 256), 1)
    col = iota((W, 256), 0)
    base = jnp.where(lane < 128, jnp.where(col < RAD, col - lane, 1), jnp.where(col >= W - RAD, col + 8 - lane, 1))
    total = jnp.zeros((ROWS, 256), F32)
    for f in range(FR):
        pick = jnp.where(base == -8 * f, 1.0, 0.0).astype(BF16)
        total = total + mm(movie[f], pick)
    packed[0] = total[:, :128].astype(BF16)
    packed[1] = total[:, 128:].astype(BF16)

    pl.semaphore_wait(barrier, N_TM - 1 + 2)
    halo = []
    for side, target in ((0, left), (1, right)):
        copy = pltpu.make_async_remote_copy(
            src_ref=packed.at[side], dst_ref=edge.at[side], send_sem=halo_s.at[side], recv_sem=halo_r.at[side],
            device_id=(target, me), device_id_type=MESH,
        )
        copy.start()
        halo.append(copy)
    om_copies = []
    for k in range(1, N_TM):
        peer = lax.rem(me + k, N_TM)
        copy = pltpu.make_async_remote_copy(
            src_ref=omega_ref.at[peer // HALF], dst_ref=om_all.at[me],
            send_sem=om_s.at[peer], recv_sem=om_r.at[me], device_id=(tile, peer), device_id_type=MESH,
        )
        copy.start()
        om_copies.append((copy, peer))
    om_all[me] = omega_ref[half]

    down = from_taps(space, iota((ROWS, ROWS), 1) - iota((ROWS, ROWS), 0) + RAD).astype(BF16)
    across = from_taps(space, iota((W, W), 0) - iota((W, W), 1) + RAD).astype(BF16)
    for f in range(FR):
        mid = mm(down, movie[f]).astype(BF16)
        far[:, f * W : (f + 1) * W] = movie[f].astype(F32) - mm(mid, across)

    n_id = iota((256, W), 0)
    c_id = iota((256, W), 1)
    j_id = lax.rem(n_id, RAD)
    spread = from_taps(space, jnp.where(n_id < 128, 136, 0) + j_id - c_id)
    owner = lax.rem(n_id, 128) // RAD

    for side in range(2):
        halo[side].wait_recv()
    rim_right = jnp.where(tile < n_tile - 1, edge[0].astype(F32), 0.0).astype(BF16)
    rim_left = jnp.where(tile > 0, edge[1].astype(F32), 0.0).astype(BF16)
    rim = mm(down, jnp.concatenate([rim_right, rim_left], axis=1)).astype(BF16)
    for f in range(FR):
        w_f = jnp.where(owner == f, spread, 0.0).astype(BF16)
        far[:, f * W : (f + 1) * W] = far[:, f * W : (f + 1) * W] - mm(rim, w_f)

    s_copies = []
    for k in (8, 7, 9, 6, 10, 5, 11, 4, 12, 3, 13, 2, 14, 1, 15, 0):
        peer = lax.rem(me + k, N_TM)
        slot = k % 2
        block = far[pl.ds(pl.multiple_of(peer * SHARE, SHARE), SHARE), :]
        for f in range(FR):
            turn[slot, pl.ds(f, SHARE, stride=FR), :] = block[:, f * W : (f + 1) * W]
        frames = turn[slot].reshape(SHARE, FR, W).astype(BF16)
        window = pl.ds(pl.multiple_of(me * FR, FR), FR)
        if k == 0:
            seen[:, window, :] = frames
        else:
            out_buf[k] = frames
            copy = pltpu.make_async_remote_copy(
                src_ref=out_buf.at[k], dst_ref=seen.at[:, window, :],
                send_sem=s_s.at[peer], recv_sem=s_r.at[me], device_id=(tile, peer), device_id_type=MESH,
            )
            copy.start()
            s_copies.append((copy, peer))

    time = time_ref[...].astype(F32)
    low = from_taps(time, iota((FRAMES, FRAMES), 1) - iota((FRAMES, FRAMES), 0) + RAD).astype(BF16)
    for k in range(1, N_TM):
        source = lax.rem(me + k, N_TM)
        pltpu.make_async_remote_copy(
            src_ref=omega_ref.at[0], dst_ref=om_all.at[source], send_sem=om_s.at[source], recv_sem=om_r.at[source],
            device_id=(tile, source), device_id_type=MESH,
        ).wait_recv()
    om = om_all[...].reshape(FRAMES, K)
    probe = om.astype(F32).T - mm_tn(om, low)
    probe2 = stacked(probe, 2)

    for k in range(1, N_TM):
        source = lax.rem(me + k, N_TM)
        pltpu.make_async_remote_copy(
            src_ref=out_buf.at[k], dst_ref=seen.at[:, pl.ds(pl.multiple_of(source * FR, FR), FR), :],
            send_sem=s_s.at[source], recv_sem=s_r.at[source], device_id=(tile, source), device_id_type=MESH,
        ).wait_recv()

    def pair(i):
        return jnp.concatenate([seen[2 * i], seen[2 * i + 1]], axis=1)

    back = jnp.zeros((3 * K, FRAMES), F32)
    for i in range(SHARE // 2):
        block = pair(i)
        y3 = stacked(fold(mm(probe2, block), 2), 3)
        y_buf[:, i * 256 : (i + 1) * 256] = y3
        back = back + mm_nt(y3, block)
    y_gram = gram(y_buf[...])
    b_mine[...] = fold(back, 3).astype(BF16)
    for i in range(4):
        g_mine[:, i * K : (i + 1) * K] = y_gram[8 * i : 8 * i + 8, :]
    b_slots[place] = b_mine[...]
    g_slots[place] = g_mine[...]
    x_copies = []
    for k in (4, 3, 5, 2, 6, 1, 7):
        other = lax.rem(place + k, HALF)
        peer = half * HALF + other
        for src, dst, ss, rs in ((b_mine, b_slots, b_s, b_r), (g_mine, g_slots, g_s, g_r)):
            copy = pltpu.make_async_remote_copy(
                src_ref=src, dst_ref=dst.at[place], send_sem=ss.at[other], recv_sem=rs.at[place],
                device_id=(tile, peer), device_id_type=MESH,
            )
            copy.start()
            x_copies.append((copy, src, dst, ss, rs, other, peer))
    for copy, src, dst, ss, rs, other, peer in x_copies:
        pltpu.make_async_remote_copy(
            src_ref=src, dst_ref=dst.at[other], send_sem=ss.at[other], recv_sem=rs.at[other],
            device_id=(tile, peer), device_id_type=MESH,
        ).wait_recv()
    g_sum = g_slots[0]
    b_sum = b_slots[0].astype(F32)
    for i in range(1, HALF):
        g_sum = g_sum + g_slots[i]
        b_sum = b_sum + b_slots[i].astype(F32)
    first = inverse_factor(jnp.concatenate([g_sum[:, i * K : (i + 1) * K] for i in range(4)], axis=0))

    back = b_sum - fold(mm_nt(stacked(b_sum, 3), low), 3)
    loads = mm(first, back, precision=HIGHEST).astype(BF16)
    probe2 = stacked(loads.astype(F32) - mm(loads, low), 2)
    down_p = jnp.zeros((FRAMES, 2 * K), F32)
    for i in range(SHARE // 2):
        block = pair(i)
        r = fold(mm(probe2, block), 2)
        r_buf[:, i * 256 : (i + 1) * 256] = r
        r3 = stacked(r, 3)
        y_buf[:, i * 256 : (i + 1) * 256] = r3
        down_p = down_p + mm_nt(block, r3[: 2 * K])
    r_gram = gram(y_buf[...])
    moved = fold_lanes(down_p, 2)
    moved = moved - fold_lanes(mm(low, stacked(moved, 2, axis=1)), 2)
    f_mine[:, :, 0:K] = moved.reshape(N_TM, FR, K)
    f_mine[:, :, K : 2 * K] = jnp.broadcast_to(r_gram[:FR][None], (N_TM, FR, K))
    f_mine[:, :, 2 * K : 3 * K] = jnp.broadcast_to(r_gram[FR:][None], (N_TM, FR, K))
    f_mine[:, :, 3 * K :] = jnp.zeros((N_TM, FR, K), F32)
    f_slots[me] = f_mine[me]
    for k in (8, 7, 9, 6, 10, 5, 11, 4, 12, 3, 13, 2, 14, 1, 15):
        peer = lax.rem(me + k, N_TM)
        pltpu.make_async_remote_copy(
            src_ref=f_mine.at[peer], dst_ref=f_slots.at[me], send_sem=f_s.at[peer], recv_sem=f_r.at[me],
            device_id=(tile, peer), device_id_type=MESH,
        ).start()
    for k in range(1, N_TM):
        source = lax.rem(me + k, N_TM)
        pltpu.make_async_remote_copy(
            src_ref=f_mine.at[source], dst_ref=f_slots.at[source], send_sem=f_s.at[source], recv_sem=f_r.at[source],
            device_id=(tile, source), device_id_type=MESH,
        ).wait()
    factors = []
    for s in range(2):
        total = f_slots[s * HALF]
        for i in range(1, HALF):
            total = total + f_slots[s * HALF + i]
        inverse = inverse_factor(jnp.concatenate([total[:, K : 2 * K], total[:, 2 * K : 3 * K]], axis=0))
        factors.append(inverse)
        coef_ref[s] = mm_nt(total[:, :K], inverse, precision=HIGHEST)
    final = jnp.where(half == 0, factors[0], factors[1]) * math.sqrt(ROWS // 2 * W)
    for i in range(SHARE // 2):
        two = mm(final, r_buf[:, i * 256 : (i + 1) * 256], precision=HIGHEST)
        for j in range(2):
            basis_ref[pl.ds(2 * i + j, K, stride=SHARE), :] = two[:, j * W : (j + 1) * W]

    for copy in halo:
        copy.wait_send()
    for copy, _ in om_copies:
        copy.wait_send()
    for copy, _ in s_copies:
        copy.wait_send()
    for entry in x_copies:
        entry[0].wait_send()


def solution(mesh):
    n_tile = mesh.shape["tile"]

    def local(movie, omega, time_taps, space_taps):
        dma = pltpu.SemaphoreType.DMA
        vmem = pl.BlockSpec(memory_space=pltpu.VMEM)
        basis, coef = pl.pallas_call(
            functools.partial(kernel, n_tile),
            out_shape=(
                jax.ShapeDtypeStruct((K * SHARE, W), F32),
                jax.ShapeDtypeStruct((2, FR, K), F32),
            ),
            in_specs=[pl.BlockSpec(memory_space=pl.ANY), vmem, vmem, vmem],
            out_specs=(vmem, vmem),
            scratch_shapes=[
                pltpu.VMEM((FR, ROWS, W), BF16),
                pltpu.VMEM((ROWS, FR * W), F32),
                pltpu.VMEM((2, ROWS, W), BF16),
                pltpu.VMEM((2, ROWS, W), BF16),
                pltpu.VMEM((2, SHARE * FR, W), F32),
                pltpu.VMEM((N_TM, SHARE, FR, W), BF16),
                pltpu.VMEM((SHARE, FRAMES, W), BF16),
                pltpu.VMEM((N_TM, FR, K), BF16),
                pltpu.VMEM((HALF, K, FRAMES), BF16),
                pltpu.VMEM((HALF, 8, 128), F32),
                pltpu.VMEM((K, FRAMES), BF16),
                pltpu.VMEM((8, 128), F32),
                pltpu.VMEM((N_TM, FR, 128), F32),
                pltpu.VMEM((N_TM, FR, 128), F32),
                pltpu.VMEM((3 * K, PIX), BF16),
                pltpu.VMEM((K, PIX), F32),
                dma(()), dma((2,)), dma((2,)), dma((N_TM,)), dma((N_TM,)), dma((N_TM,)), dma((N_TM,)),
                dma((HALF,)), dma((HALF,)), dma((HALF,)), dma((HALF,)), dma((N_TM,)), dma((N_TM,)),
            ],
            compiler_params=pltpu.CompilerParams(collective_id=0, has_side_effects=True),
            name="low_rank",
        )(
            movie,
            jnp.transpose(omega[:, 0], (0, 2, 1)),
            time_taps.reshape(1, -1),
            space_taps.reshape(1, -1),
        )
        return basis.reshape(K, SHARE, W), jnp.transpose(coef, (0, 2, 1))[:, None]

    in_specs = (P("tm", None, "tile"), P(None, "tile", None, "tm"), P(), P())
    out_specs = (P(None, "tm", "tile"), P(None, "tile", None, "tm"))
    return jax.shard_map(local, mesh=mesh, in_specs=in_specs, out_specs=out_specs, check_vma=False)
```

time: 343 us -> 69.1 us (0.20)
  waiting for transfers between devices: 256 us -> 0 us
  Pallas kernels: 0 us -> 65.9 us
  matrix products: 27.9 us -> 0 us
  other arithmetic: 24.2 us -> 0 us
  starting transfers between devices: 14.6 us -> 0 us
  between operations: 14.3 us -> 0.65 us
    psum x2 -> x0, waiting for transfers between devices: 248 us -> none  [subspace(): lax.psum(partial_value.astype(jnp.bfloat16), 'tm').astype(jnp.float32)]
    pallas_call x0 -> x1, Pallas kernels: none -> 65.9 us  [local(): pl.pallas_call(functools.partial(kernel, n_tile), out_shape=(jax.ShapeDty...]
    another operation x12 -> x0, other arithmetic: 22.2 us -> none  [the longest x7 12.2 us: orthonormal(): factor_low = jnp.linalg.cholesky(gram_block)]
    dot_general x7 -> x0, matrix products: 19.3 us -> none  [the longest x2 6.08 us: orthonormal(): gram_block = jnp.dot(matrix, matrix.T, precision=lax.Precision.HIGHEST)]
    ppermute x4 -> x0, starting transfers between devices: 14.5 us -> none  [the longest x2 8.51 us: with_halo(): lax.ppermute(lax.slice_in_dim(block, block.shape[dim] - width, None, axis...]
    another operation x2 -> x0, matrix products: 8.65 us -> none  [orthonormal(): return jax.scipy.linalg.solve_triangular(factor_low, matrix, lower=True)]
    ppermute x4 -> x0, waiting for transfers between devices: 8.36 us -> none  [the longest x2 7.9 us: with_halo(): lax.ppermute(lax.slice_in_dim(block, 0, width, axis=dim), axis, backward)]
  transfers between devices with their start and end apart: 6 -> 0, of which waited for: 5 -> 0; matrix products, arithmetic and copies ran while one was open for 0% -> 0% of each run, Pallas kernels for 0% -> 0%
where the time goes in v1:
time: 69.1 us; the launch traced here: 68.8 us
  Pallas kernels  65.9 us (95%)
  local copies, waits for them, and re-layouts  2.28 us (3%)
    pallas_call x1, Pallas kernels, local(): pl.pallas_call(functools.partial(kernel, n_tile), out_shape=(jax.ShapeDty...  65.9 us
    unnamed x4, local copies, waits for them, and re-layouts  2.28 us

profile of v1, /device:TPU:1, one launch (start us, length us, event | category | flops | bytes accessed | tf_op | source)
XLA Modules:
  0.0 68.8 jit_solution(5133276647664586412)
XLA Ops:
  0.6 65.9 %low_rank.1 = (f32[512,128]{1,0:T(8,128)}, f32[2,16,32]{2,1,0:T(8,128)}) custom-call(bf16[16,256,128]{2,1,0:T(8,128)(2,1)} %movie_hbm.1, bf16[2,16,32]{2,1,0:T(8,128)(2,1)} %bitcast.13, bf16[1,17]{1,0:T(2,128)(2,1)} %bitcast.14, bf16[1,17]{1,0:T(2,128)(2,1)} %bitcast.15), custom_call_target="tpu_custom_call" | custom-call | tf_op jit(solution)/shard_map/low_rank/pallas_call | solution.py:312
  66.5 0.0 copy-start
  66.6 1.7 %copy.9 = f32[32,16,128]{2,1,0:T(8,128)} copy(f32[32,16,128]{2,1,0:T(8,128)} %bitcast.11) | data formatting | bytes 524288
  68.2 0.0 copy-done
  68.2 0.6 copy.10
Async XLA Ops:
  66.5 1.7 %copy-start = (f32[2,16,32]{2,1,0:T(8,128)S(1)}, f32[2,16,32]{2,1,0:T(8,128)}, u32[]{:S(2)}) copy-start(f32[2,16,32]{2,1,0:T(8,128)} %get-tuple-element.5) | copy-start | bytes 12292

commit v2 on v1

v2 whole, which is shorter than its diff:
```python
import functools
import math

import jax
import jax.numpy as jnp
from jax import lax
from jax.experimental import pallas as pl
from jax.experimental.pallas import tpu as pltpu
from jax.sharding import PartitionSpec as P

MESH = pl.DeviceIdType.MESH
F32 = jnp.float32
BF16 = jnp.bfloat16
HIGHEST = lax.Precision.HIGHEST

N_TM = 16
HALF = 8
FR = 16
FRAMES = 256
ROWS = 256
SHARE = 16
W = 128
K = 32
RAD = 8
PIX = SHARE * W


def mm(a, b, **kw):
    return jnp.dot(a, b, preferred_element_type=F32, **kw)


def mm_nt(a, b, **kw):
    return lax.dot_general(a, b, (((1,), (1,)), ((), ())), preferred_element_type=F32, **kw)


def mm_tn(a, b, **kw):
    return lax.dot_general(a, b, (((0,), (0,)), ((), ())), preferred_element_type=F32, **kw)


def pieces(x, count):
    out = []
    for _ in range(count - 1):
        part = x.astype(BF16)
        out.append(part)
        x = x - part.astype(F32)
    out.append(x.astype(BF16))
    return out


def stacked(x, count, axis=0):
    return jnp.concatenate(pieces(x, count), axis=axis)


def fold(x, count):
    total = x[:K]
    for i in range(1, count):
        total = total + x[i * K : (i + 1) * K]
    return total


def fold_lanes(x, count):
    total = x[:, :K]
    for i in range(1, count):
        total = total + x[:, i * K : (i + 1) * K]
    return total


def iota(shape, dim):
    return lax.broadcasted_iota(jnp.int32, shape, dim)


def from_taps(taps, index):
    out = jnp.zeros(index.shape, F32)
    for k in range(2 * RAD + 1):
        out = jnp.where(index == k, taps[:, k : k + 1], out)
    return out


def gram(x3):
    return fold_lanes(fold(mm_nt(x3, x3), 3), 3)


def inverse_factors(grams):
    row = iota((8, 128), 0)
    eye = jnp.where(iota((K, K), 0) == iota((K, K), 1), 1.0, 0.0)
    state = []
    for g in grams:
        aug = jnp.concatenate([g, eye, jnp.zeros((K, 64), F32)], axis=1)
        state.append(([aug[8 * i : 8 * i + 8] for i in range(4)], []))
    for b in range(4):
        spread = [
            [[jnp.broadcast_to(aug[i][:, 8 * b + t : 8 * b + t + 1], (8, 128)) for i in range(b, 4)] for t in range(8)]
            for aug, _ in state
        ]
        scale = [jnp.ones((8, 128), F32) for _ in state]
        for t in range(8):
            for n, (aug, _) in enumerate(state):
                cols = spread[n]
                pivot = cols[t][0][t : t + 1, :]
                inverse = 1.0 / pivot
                scale[n] = jnp.where(row == t, pivot, scale[n])
                line = aug[b][t : t + 1, :] * inverse
                heads = [cols[u][0][t : t + 1, :] * inverse for u in range(t + 1, 8)]
                for i in range(b, 4):
                    factor = cols[t][i - b]
                    if i == b:
                        factor = jnp.where(row > t, factor, 0.0)
                    aug[i] = aug[i] - factor * line
                    for u in range(t + 1, 8):
                        cols[u][i - b] = cols[u][i - b] - factor * heads[u - t - 1]
        for n, (aug, done) in enumerate(state):
            done.append(aug[b] * lax.rsqrt(scale[n]))
    return [jnp.concatenate(done, axis=0)[:, K : 2 * K] for _, done in state]


def toeplitz(taps, size, flip):
    lane, row = iota((8, size), 1), iota((8, size), 0)
    head = from_taps(taps, row + 2 * RAD - lane if flip else lane - row)
    rows = []
    for i in range(size // 8):
        block = head
        if i == 0:
            block = jnp.where(lane >= 8, head, 0.0)
        if i == size // 8 - 1:
            block = jnp.where(lane < 16, head, 0.0)
        shift = (8 * i - 8) % size
        rows.append(pltpu.roll(block, shift, 1) if shift else block)
    return jnp.concatenate(rows, axis=0).astype(BF16)


def zeros16(*shape):
    return jnp.zeros(shape, BF16)


def pack_gram(ref, g):
    for i in range(4):
        ref[:, i * K : (i + 1) * K] = g[8 * i : 8 * i + 8, :]


def unpack_gram(total):
    return jnp.concatenate([total[:, i * K : (i + 1) * K] for i in range(4)], axis=0)


def kernel(
    n_tile,
    movie_hbm, omega_hbm, time_hbm, space_hbm,
    basis_ref, coef_ref,
    movie, omega_ref, time_ref, space_ref, far, packed, edge, turn, out_buf, seen, om_all,
    b_slots, g_slots, b_mine, g_mine, h_mine, h_slots, d_mine, d_slots, y_buf, r_buf,
    load_sem, halo_s, halo_r, s_s, s_r, om_s, om_r, b_s, b_r, g_s, g_r, h_s, h_r, d_s, d_r,
):
    tile = lax.axis_index("tile")
    me = lax.axis_index("tm")
    half = me // HALF
    place = me - half * HALF
    left = lax.rem(tile + n_tile - 1, n_tile)
    right = lax.rem(tile + 1, n_tile)
    far_first = (8, 7, 9, 6, 10, 5, 11, 4, 12, 3, 13, 2, 14, 1, 15)

    loads = [
        pltpu.make_async_copy(src, dst, load_sem.at[i])
        for i, (src, dst) in enumerate(
            ((movie_hbm, movie), (space_hbm, space_ref), (time_hbm, time_ref), (omega_hbm, omega_ref))
        )
    ]
    for load in loads:
        load.start()
    barrier = pltpu.get_barrier_semaphore()
    for k in far_first:
        pl.semaphore_signal(barrier, inc=1, device_id=(tile, lax.rem(me + k, N_TM)), device_id_type=MESH)
    pl.semaphore_signal(barrier, inc=1, device_id=(left, me), device_id_type=MESH)
    pl.semaphore_signal(barrier, inc=1, device_id=(right, me), device_id_type=MESH)

    loads[1].wait()
    space = space_ref[...].astype(F32)
    down = toeplitz(space, ROWS, False)
    side = toeplitz(space, W, True)
    across = jnp.concatenate(
        [jnp.concatenate([side, zeros16(W, W)], axis=1), jnp.concatenate([zeros16(W, W), side], axis=1)], axis=0
    )
    lane8, row8 = iota((8, W), 1), iota((8, W), 0)
    none8 = jnp.zeros((8, W), F32)
    rims = []
    for offset in (136, 0):
        one = from_taps(space, offset + row8 - lane8)
        rims.append(
            jnp.concatenate(
                [jnp.concatenate([one, none8], axis=1), jnp.concatenate([none8, one], axis=1)], axis=0
            ).astype(BF16)
        )
    unit = jnp.where(lane8 == row8, 1.0, 0.0)
    picks = []
    for f in range(FR):
        moved = pltpu.roll(unit, 8 * f, 1) if f else unit
        top = jnp.concatenate([moved, none8], axis=0).astype(BF16)
        bottom = jnp.concatenate([none8, moved], axis=0).astype(BF16)
        picks.append(jnp.concatenate([top, zeros16(16, W)], axis=1))
        picks.append(zeros16(W - 32, 2 * W))
        picks.append(jnp.concatenate([zeros16(16, W), bottom], axis=1))
    loads[0].wait()

    def frames2(g):
        return jnp.concatenate([movie[2 * g], movie[2 * g + 1]], axis=1)

    total = mm(jnp.concatenate([movie[f] for f in range(FR)], axis=1), jnp.concatenate(picks, axis=0))
    packed[0] = total[:, :W].astype(BF16)
    packed[1] = total[:, W:].astype(BF16)

    pl.semaphore_wait(barrier, N_TM - 1 + 2)
    halo = []
    for i, target in ((0, left), (1, right)):
        copy = pltpu.make_async_remote_copy(
            src_ref=packed.at[i], dst_ref=edge.at[i], send_sem=halo_s.at[i], recv_sem=halo_r.at[i],
            device_id=(target, me), device_id_type=MESH,
        )
        copy.start()
        halo.append(copy)

    for g in range(FR // 2):
        two = frames2(g)
        mid = mm(down, two).astype(BF16)
        far[:, 2 * g * W : 2 * (g + 1) * W] = two.astype(F32) - mm(mid, across)

    loads[2].wait()
    loads[3].wait()
    om_copies = []
    for k in far_first:
        peer = lax.rem(me + k, N_TM)
        copy = pltpu.make_async_remote_copy(
            src_ref=omega_ref.at[peer // HALF], dst_ref=om_all.at[me],
            send_sem=om_s.at[peer], recv_sem=om_r.at[me], device_id=(tile, peer), device_id_type=MESH,
        )
        copy.start()
        om_copies.append((copy, peer))
    om_all[me] = omega_ref[half]

    for i in range(2):
        halo[i].wait_recv()
    rim_right = jnp.where(tile < n_tile - 1, edge[0].astype(F32), 0.0).astype(BF16)
    rim_left = jnp.where(tile > 0, edge[1].astype(F32), 0.0).astype(BF16)
    rim = mm(down, jnp.concatenate([rim_right, rim_left], axis=1)).astype(BF16)
    for g in range(FR // 2):
        rows = []
        for i in range(2):
            rows += [zeros16(16 * g, 2 * W)] if g else []
            rows += [rims[i]]
            rows += [zeros16(W - 16 * g - 16, 2 * W)] if g < FR // 2 - 1 else []
        window = slice(2 * g * W, 2 * (g + 1) * W)
        far[:, window] = far[:, window] - mm(rim, jnp.concatenate(rows, axis=0))

    s_copies = []
    for k in far_first + (0,):
        peer = lax.rem(me + k, N_TM)
        slot = k % 2
        block = far[pl.ds(pl.multiple_of(peer * SHARE, SHARE), SHARE), :]
        for f in range(FR):
            turn[slot, pl.ds(f, SHARE, stride=FR), :] = block[:, f * W : (f + 1) * W]
        frames = turn[slot].reshape(SHARE, FR, W).astype(BF16)
        window = pl.ds(pl.multiple_of(me * FR, FR), FR)
        if k == 0:
            seen[:, window, :] = frames
        else:
            out_buf[k] = frames
            copy = pltpu.make_async_remote_copy(
                src_ref=out_buf.at[k], dst_ref=seen.at[:, window, :],
                send_sem=s_s.at[peer], recv_sem=s_r.at[me], device_id=(tile, peer), device_id_type=MESH,
            )
            copy.start()
            s_copies.append((copy, peer))

    time = time_ref[...].astype(F32)
    low = toeplitz(time, FRAMES, False)
    for k in range(1, N_TM):
        source = lax.rem(me + k, N_TM)
        pltpu.make_async_remote_copy(
            src_ref=omega_ref.at[0], dst_ref=om_all.at[source], send_sem=om_s.at[source], recv_sem=om_r.at[source],
            device_id=(tile, source), device_id_type=MESH,
        ).wait_recv()
    om = om_all[...].reshape(FRAMES, K)
    probe = om.astype(F32).T - mm_tn(om, low)
    probe2 = stacked(probe, 2)

    for k in range(1, N_TM):
        source = lax.rem(me + k, N_TM)
        pltpu.make_async_remote_copy(
            src_ref=out_buf.at[k], dst_ref=seen.at[:, pl.ds(pl.multiple_of(source * FR, FR), FR), :],
            send_sem=s_s.at[source], recv_sem=s_r.at[source], device_id=(tile, source), device_id_type=MESH,
        ).wait_recv()

    def pair(i):
        return jnp.concatenate([seen[2 * i], seen[2 * i + 1]], axis=1)

    for i in range(SHARE // 2):
        y_buf[:, i * 256 : (i + 1) * 256] = stacked(fold(mm(probe2, pair(i)), 2), 3)
    pack_gram(g_mine, gram(y_buf[...]))
    x_copies = []

    def to_half(src, dst, ss, rs):
        dst[place] = src[...]
        for k in (4, 3, 5, 2, 6, 1, 7):
            other = lax.rem(place + k, HALF)
            copy = pltpu.make_async_remote_copy(
                src_ref=src, dst_ref=dst.at[place], send_sem=ss.at[other], recv_sem=rs.at[place],
                device_id=(tile, half * HALF + other), device_id_type=MESH,
            )
            copy.start()
            x_copies.append(copy)

    def from_half(src, dst, ss, rs):
        for k in range(1, HALF):
            other = lax.rem(place + k, HALF)
            pltpu.make_async_remote_copy(
                src_ref=src, dst_ref=dst.at[other], send_sem=ss.at[other], recv_sem=rs.at[other],
                device_id=(tile, half * HALF + other), device_id_type=MESH,
            ).wait_recv()

    to_half(g_mine, g_slots, g_s, g_r)
    back = jnp.zeros((3 * K, FRAMES), F32)
    for i in range(SHARE // 2):
        back = back + mm_nt(y_buf[:, i * 256 : (i + 1) * 256], pair(i))
    b_mine[...] = fold(back, 3).astype(BF16)
    to_half(b_mine, b_slots, b_s, b_r)
    from_half(g_mine, g_slots, g_s, g_r)
    g_sum = g_slots[0]
    for i in range(1, HALF):
        g_sum = g_sum + g_slots[i]
    first = inverse_factors([unpack_gram(g_sum)])[0]
    from_half(b_mine, b_slots, b_s, b_r)
    b_sum = b_slots[0].astype(F32)
    for i in range(1, HALF):
        b_sum = b_sum + b_slots[i].astype(F32)

    back = b_sum - fold(mm_nt(stacked(b_sum, 3), low), 3)
    loadings = mm(first, back, precision=HIGHEST).astype(BF16)
    probe2 = stacked(loadings.astype(F32) - mm(loadings, low), 2)
    for i in range(SHARE // 2):
        r = fold(mm(probe2, pair(i)), 2)
        r_buf[:, i * 256 : (i + 1) * 256] = r
        y_buf[:, i * 256 : (i + 1) * 256] = stacked(r, 3)
    pack_gram(h_mine, gram(y_buf[...]))

    def to_all(src, dst, ss, rs):
        for k in far_first:
            peer = lax.rem(me + k, N_TM)
            copy = pltpu.make_async_remote_copy(
                src_ref=src(peer), dst_ref=dst.at[me], send_sem=ss.at[peer], recv_sem=rs.at[me],
                device_id=(tile, peer), device_id_type=MESH,
            )
            copy.start()
            x_copies.append(copy)

    def from_all(src, dst, ss, rs):
        for k in range(1, N_TM):
            source = lax.rem(me + k, N_TM)
            pltpu.make_async_remote_copy(
                src_ref=src(source), dst_ref=dst.at[source], send_sem=ss.at[source], recv_sem=rs.at[source],
                device_id=(tile, source), device_id_type=MESH,
            ).wait_recv()

    to_all(lambda peer: h_mine, h_slots, h_s, h_r)
    h_slots[me] = h_mine[...]
    down_p = jnp.zeros((FRAMES, 2 * K), F32)
    for i in range(SHARE // 2):
        down_p = down_p + mm_nt(pair(i), y_buf[: 2 * K, i * 256 : (i + 1) * 256])
    moved = fold_lanes(down_p, 2)
    moved = moved - fold_lanes(mm(low, stacked(moved, 2, axis=1)), 2)
    d_mine[...] = moved.astype(BF16).reshape(N_TM, FR, K)
    to_all(lambda peer: d_mine.at[peer], d_slots, d_s, d_r)
    d_slots[me] = d_mine[me]
    from_all(lambda peer: h_mine, h_slots, h_s, h_r)
    grams = []
    for s in range(2):
        total = h_slots[s * HALF]
        for i in range(1, HALF):
            total = total + h_slots[s * HALF + i]
        grams.append(unpack_gram(total))
    factors = inverse_factors(grams)
    final = jnp.where(half == 0, factors[0], factors[1])
    for i in range(SHARE // 2):
        two = mm(final, r_buf[:, i * 256 : (i + 1) * 256], precision=HIGHEST)
        for j in range(2):
            basis_ref[pl.ds(2 * i + j, K, stride=SHARE), :] = two[:, j * W : (j + 1) * W]
    from_all(lambda peer: d_mine.at[peer], d_slots, d_s, d_r)
    scale = 1.0 / math.sqrt(ROWS // 2 * W)
    for s in range(2):
        total = d_slots[s * HALF].astype(F32)
        for i in range(1, HALF):
            total = total + d_slots[s * HALF + i].astype(F32)
        coef_ref[s] = mm_nt(total, factors[s], precision=HIGHEST) * scale

    for copy in halo:
        copy.wait_send()
    for copy, _ in om_copies:
        copy.wait_send()
    for copy, _ in s_copies:
        copy.wait_send()
    for copy in x_copies:
        copy.wait_send()


def solution(mesh):
    n_tile = mesh.shape["tile"]

    def local(movie, omega, time_taps, space_taps):
        dma = pltpu.SemaphoreType.DMA
        vmem = pl.BlockSpec(memory_space=pltpu.VMEM)
        basis, coef = pl.pallas_call(
            functools.partial(kernel, n_tile),
            out_shape=(
                jax.ShapeDtypeStruct((K * SHARE, W), F32),
                jax.ShapeDtypeStruct((2, FR, K), F32),
            ),
            in_specs=[pl.BlockSpec(memory_space=pl.ANY)] * 4,
            out_specs=(vmem, vmem),
            scratch_shapes=[
                pltpu.VMEM((FR, ROWS, W), BF16),
                pltpu.VMEM((2, FR, K), BF16),
                pltpu.VMEM((1, 2 * RAD + 1), BF16),
                pltpu.VMEM((1, 2 * RAD + 1), BF16),
                pltpu.VMEM((ROWS, FR * W), F32),
                pltpu.VMEM((2, ROWS, W), BF16),
                pltpu.VMEM((2, ROWS, W), BF16),
                pltpu.VMEM((2, SHARE * FR, W), F32),
                pltpu.VMEM((N_TM, SHARE, FR, W), BF16),
                pltpu.VMEM((SHARE, FRAMES, W), BF16),
                pltpu.VMEM((N_TM, FR, K), BF16),
                pltpu.VMEM((HALF, K, FRAMES), BF16),
                pltpu.VMEM((HALF, 8, 128), F32),
                pltpu.VMEM((K, FRAMES), BF16),
                pltpu.VMEM((8, 128), F32),
                pltpu.VMEM((8, 128), F32),
                pltpu.VMEM((N_TM, 8, 128), F32),
                pltpu.VMEM((N_TM, FR, K), BF16),
                pltpu.VMEM((N_TM, FR, K), BF16),
                pltpu.VMEM((3 * K, PIX), BF16),
                pltpu.VMEM((K, PIX), F32),
                dma((4,)), dma((2,)), dma((2,)), dma((N_TM,)), dma((N_TM,)), dma((N_TM,)), dma((N_TM,)),
                dma((HALF,)), dma((HALF,)), dma((HALF,)), dma((HALF,)),
                dma((N_TM,)), dma((N_TM,)), dma((N_TM,)), dma((N_TM,)),
            ],
            compiler_params=pltpu.CompilerParams(collective_id=0, has_side_effects=True),
            name="low_rank",
        )(
            movie,
            jnp.transpose(omega[:, 0], (0, 2, 1)),
            time_taps.reshape(1, -1),
            space_taps.reshape(1, -1),
        )
        scale = math.sqrt(ROWS // 2 * W)
        return basis.reshape(K, SHARE, W) * scale, jnp.transpose(coef * scale, (0, 2, 1))[:, None]

    in_specs = (P("tm", None, "tile"), P(None, "tile", None, "tm"), P(), P())
    out_specs = (P(None, "tm", "tile"), P(None, "tile", None, "tm"))
    return jax.shard_map(local, mesh=mesh, in_specs=in_specs, out_specs=out_specs, check_vma=False)
```

time: 69.1 us -> 63.6 us (0.920)
  Pallas kernels: 65.9 us -> 60.5 us
  other arithmetic: 0 us -> 2.28 us
  local copies, waits for them, and re-layouts: 2.28 us -> 0.01 us
    pallas_call x1, Pallas kernels: 65.9 us -> 60.5 us  [local(): pl.pallas_call(functools.partial(kernel, n_tile), out_shape=(jax.ShapeDty...]
    unnamed x4 -> x2, local copies, waits for them, and re-layouts: 2.28 us -> 0.01 us
    mul x0 -> x1, other arithmetic: none -> 1.68 us  [local(): basis.reshape(K, SHARE, W) * scale]
where the time goes in v2:
time: 63.6 us; the launch traced here: 63.4 us
  Pallas kernels  60.5 us (95%)
  other arithmetic  2.28 us (4%)
  between operations  0.65 us (1%)
    pallas_call x1, Pallas kernels, local(): pl.pallas_call(functools.partial(kernel, n_tile), out_shape=(jax.ShapeDty...  60.5 us
    mul x1, other arithmetic, local(): basis.reshape(K, SHARE, W) * scale  1.68 us

profile of v2, /device:TPU:1, one launch (start us, length us, event | category | flops | bytes accessed | tf_op | source)
XLA Modules:
  0.0 63.4 jit_solution(4824511784576498661)
XLA Ops:
  0.6 60.5 %low_rank.1 = (f32[512,128]{1,0:T(8,128)}, f32[2,16,32]{2,1,0:T(8,128)}) custom-call(bf16[16,256,128]{2,1,0:T(8,128)(2,1)} %movie_hbm.1, bf16[2,16,32]{2,1,0:T(8,128)(2,1)} %bitcast.13, bf16[1,17]{1,0:T(2,128)(2,1)} %bitcast.14, bf16[1,17]{1,0:T(2,128)(2,1)} %bitcast.15), custom_call_target="tpu_custom_call" | custom-call | tf_op jit(solution)/shard_map/low_rank/pallas_call | solution.py:407
  61.1 0.0 copy-start
  61.1 1.7 %broadcast_multiply_fusion = f32[512,128]{1,0:T(8,128)} fusion(f32[512,128]{1,0:T(8,128)} %get-tuple-element.4), kind=kLoop, calls=%fused_computation | loop fusion | flops 65536 | bytes 524288 | tf_op jit(solution)/shard_map/mul | solution.py:450
  62.8 0.0 copy-done
  62.8 0.6 multiply_bitcast_fusion
Async XLA Ops:
  61.1 1.7 %copy-start = (f32[2,16,32]{2,1,0:T(8,128)S(1)}, f32[2,16,32]{2,1,0:T(8,128)}, u32[]{:S(2)}) copy-start(f32[2,16,32]{2,1,0:T(8,128)} %get-tuple-element.5) | copy-start | bytes 12292

commit v3 on v2

--- a/solution.py
+++ b/solution.py
@@ -23,6 +23,7 @@
 K = 32
 RAD = 8
 PIX = SHARE * W
+EARLY = (8, 7)
 
 
 def mm(a, b, **kw):
@@ -145,9 +146,9 @@
     n_tile,
     movie_hbm, omega_hbm, time_hbm, space_hbm,
     basis_ref, coef_ref,
-    movie, omega_ref, time_ref, space_ref, far, packed, edge, turn, out_buf, seen, om_all,
+    movie, omega_ref, om_mine, fix, rim_buf, share, time_ref, space_ref, far, packed, edge, turn, out_buf, seen, om_all,
     b_slots, g_slots, b_mine, g_mine, h_mine, h_slots, d_mine, d_slots, y_buf, r_buf,
-    load_sem, halo_s, halo_r, s_s, s_r, om_s, om_r, b_s, b_r, g_s, g_r, h_s, h_r, d_s, d_r,
+    load_sem, halo_s, halo_r, s_s, s_r, om_s, om_r, c_s, c_r, b_s, b_r, g_s, g_r, h_s, h_r, d_s, d_r,
 ):
     tile = lax.axis_index("tile")
     me = lax.axis_index("tm")
@@ -206,6 +207,37 @@
     packed[0] = total[:, :W].astype(BF16)
     packed[1] = total[:, W:].astype(BF16)
 
+    for g in range(FR // 2):
+        two = frames2(g)
+        mid = mm(down, two).astype(BF16)
+        far[:, 2 * g * W : 2 * (g + 1) * W] = two.astype(F32) - mm(mid, across)
+
+
+    def rows_of(values, slot):
+        for f in range(FR):
+            turn[slot, pl.ds(f, SHARE, stride=FR), :] = values[:, f * W : (f + 1) * W]
+        return turn[slot].reshape(SHARE, FR, W)
+
+    def rows_at(peer):
+        return pl.ds(pl.multiple_of(peer * SHARE, SHARE), SHARE)
+
+    s_copies = []
+
+    def block_copy(k):
+        peer = lax.rem(me + k, N_TM)
+        return pltpu.make_async_remote_copy(
+            src_ref=out_buf.at[k], dst_ref=seen.at[:, rows_at(me), :],
+            send_sem=s_s.at[peer], recv_sem=s_r.at[me], device_id=(tile, peer), device_id_type=MESH,
+        )
+
+    for i, k in enumerate(EARLY):
+        out_buf[k] = rows_of(far[rows_at(lax.rem(me + k, N_TM)), :], i % 2).astype(BF16)
+    loads[2].wait()
+    loads[3].wait()
+    for i in range(2):
+        some = omega_ref[i].astype(F32)
+        om_mine[i] = jnp.concatenate([some[4 * a : 4 * a + 4] for a in range(4)], axis=1).astype(BF16)
+
     pl.semaphore_wait(barrier, N_TM - 1 + 2)
     halo = []
     for i, target in ((0, left), (1, right)):
@@ -215,77 +247,95 @@
         )
         copy.start()
         halo.append(copy)
-
-    for g in range(FR // 2):
-        two = frames2(g)
-        mid = mm(down, two).astype(BF16)
-        far[:, 2 * g * W : 2 * (g + 1) * W] = two.astype(F32) - mm(mid, across)
-
-    loads[2].wait()
-    loads[3].wait()
+    for k in EARLY:
+        s_copies.append(block_copy(k))
+        s_copies[-1].start()
     om_copies = []
     for k in far_first:
         peer = lax.rem(me + k, N_TM)
         copy = pltpu.make_async_remote_copy(
-            src_ref=omega_ref.at[peer // HALF], dst_ref=om_all.at[me],
+            src_ref=om_mine.at[peer // HALF], dst_ref=om_all.at[me],
             send_sem=om_s.at[peer], recv_sem=om_r.at[me], device_id=(tile, peer), device_id_type=MESH,
         )
         copy.start()
-        om_copies.append((copy, peer))
-    om_all[me] = omega_ref[half]
+        om_copies.append(copy)
+    om_all[me] = om_mine[half]
 
     for i in range(2):
         halo[i].wait_recv()
     rim_right = jnp.where(tile < n_tile - 1, edge[0].astype(F32), 0.0).astype(BF16)
     rim_left = jnp.where(tile > 0, edge[1].astype(F32), 0.0).astype(BF16)
     rim = mm(down, jnp.concatenate([rim_right, rim_left], axis=1)).astype(BF16)
-    for g in range(FR // 2):
+    rim_buf[...] = rim
+    c_copies = []
+    for i, k in enumerate(EARLY):
+        peer = lax.rem(me + k, N_TM)
+        copy = pltpu.make_async_remote_copy(
+            src_ref=rim_buf.at[rows_at(peer), :], dst_ref=fix.at[i],
+            send_sem=c_s.at[i], recv_sem=c_r.at[i], device_id=(tile, peer), device_id_type=MESH,
+        )
+        copy.start()
+        c_copies.append(copy)
+
+    def rim_matrix(g):
         rows = []
         for i in range(2):
             rows += [zeros16(16 * g, 2 * W)] if g else []
             rows += [rims[i]]
             rows += [zeros16(W - 16 * g - 16, 2 * W)] if g < FR // 2 - 1 else []
+        return jnp.concatenate(rows, axis=0)
+
+    for g in range(FR // 2):
         window = slice(2 * g * W, 2 * (g + 1) * W)
-        far[:, window] = far[:, window] - mm(rim, jnp.concatenate(rows, axis=0))
-
-    s_copies = []
+        far[:, window] = far[:, window] - mm(rim, rim_matrix(g))
+
     for k in far_first + (0,):
-        peer = lax.rem(me + k, N_TM)
-        slot = k % 2
-        block = far[pl.ds(pl.multiple_of(peer * SHARE, SHARE), SHARE), :]
-        for f in range(FR):
-            turn[slot, pl.ds(f, SHARE, stride=FR), :] = block[:, f * W : (f + 1) * W]
-        frames = turn[slot].reshape(SHARE, FR, W).astype(BF16)
-        window = pl.ds(pl.multiple_of(me * FR, FR), FR)
+        if k in EARLY:
+            continue
+        block = rows_of(far[rows_at(lax.rem(me + k, N_TM)), :], k % 2).astype(BF16)
         if k == 0:
-            seen[:, window, :] = frames
+            seen[:, rows_at(me), :] = block
         else:
-            out_buf[k] = frames
-            copy = pltpu.make_async_remote_copy(
-                src_ref=out_buf.at[k], dst_ref=seen.at[:, window, :],
-                send_sem=s_s.at[peer], recv_sem=s_r.at[me], device_id=(tile, peer), device_id_type=MESH,
-            )
-            copy.start()
-            s_copies.append((copy, peer))
+            out_buf[k] = block
+            s_copies.append(block_copy(k))
+            s_copies[-1].start()
 
     time = time_ref[...].astype(F32)
     low = toeplitz(time, FRAMES, False)
     for k in range(1, N_TM):
         source = lax.rem(me + k, N_TM)
         pltpu.make_async_remote_copy(
-            src_ref=omega_ref.at[0], dst_ref=om_all.at[source], send_sem=om_s.at[source], recv_sem=om_r.at[source],
+            src_ref=om_mine.at[0], dst_ref=om_all.at[source], send_sem=om_s.at[source], recv_sem=om_r.at[source],
             device_id=(tile, source), device_id_type=MESH,
         ).wait_recv()
-    om = om_all[...].reshape(FRAMES, K)
-    probe = om.astype(F32).T - mm_tn(om, low)
+    om = om_all[...].astype(F32).reshape(4 * N_TM, 128)
+    om = jnp.concatenate([om[:, a * K : (a + 1) * K] for a in range(4)], axis=0).astype(BF16)
+    n_id = iota((FRAMES, FRAMES), 0)
+    at = lax.rem(n_id, 64) // 4 * FR + n_id // 64 * 4 + lax.rem(n_id, 4)
+    om = mm_tn(om, jnp.where(at == iota((FRAMES, FRAMES), 1), 1.0, 0.0).astype(BF16))
+    probe = om - mm(om.astype(BF16), low)
     probe2 = stacked(probe, 2)
 
-    for k in range(1, N_TM):
-        source = lax.rem(me + k, N_TM)
+    def block_wait(k):
+        source = lax.rem(me + N_TM - k, N_TM)
         pltpu.make_async_remote_copy(
-            src_ref=out_buf.at[k], dst_ref=seen.at[:, pl.ds(pl.multiple_of(source * FR, FR), FR), :],
+            src_ref=out_buf.at[k], dst_ref=seen.at[:, rows_at(source), :],
             send_sem=s_s.at[source], recv_sem=s_r.at[source], device_id=(tile, source), device_id_type=MESH,
         ).wait_recv()
+
+    for copy in c_copies:
+        copy.wait_recv()
+    rims_in = fix[...].reshape(len(EARLY) * SHARE, 2 * W)
+    for g in range(FR // 2):
+        share[:, 2 * g * W : 2 * (g + 1) * W] = mm(rims_in, rim_matrix(g))
+    for i, k in enumerate(EARLY):
+        block_wait(k)
+        window = rows_at(lax.rem(me + N_TM - k, N_TM))
+        moved = rows_of(share[i * SHARE : (i + 1) * SHARE, :], i % 2)
+        seen[:, window, :] = (seen[:, window, :].astype(F32) - moved).astype(BF16)
+    for k in far_first:
+        if k not in EARLY:
+            block_wait(k)
 
     def pair(i):
         return jnp.concatenate([seen[2 * i], seen[2 * i + 1]], axis=1)
@@ -375,24 +425,21 @@
             total = total + h_slots[s * HALF + i]
         grams.append(unpack_gram(total))
     factors = inverse_factors(grams)
-    final = jnp.where(half == 0, factors[0], factors[1])
+    final = jnp.where(half == 0, factors[0], factors[1]) * math.sqrt(ROWS // 2 * W)
     for i in range(SHARE // 2):
         two = mm(final, r_buf[:, i * 256 : (i + 1) * 256], precision=HIGHEST)
         for j in range(2):
             basis_ref[pl.ds(2 * i + j, K, stride=SHARE), :] = two[:, j * W : (j + 1) * W]
     from_all(lambda peer: d_mine.at[peer], d_slots, d_s, d_r)
-    scale = 1.0 / math.sqrt(ROWS // 2 * W)
     for s in range(2):
         total = d_slots[s * HALF].astype(F32)
         for i in range(1, HALF):
             total = total + d_slots[s * HALF + i].astype(F32)
-        coef_ref[s] = mm_nt(total, factors[s], precision=HIGHEST) * scale
+        coef_ref[s] = mm_nt(total, factors[s], precision=HIGHEST)
 
     for copy in halo:
         copy.wait_send()
-    for copy, _ in om_copies:
-        copy.wait_send()
-    for copy, _ in s_copies:
+    for copy in om_copies + s_copies + c_copies:
         copy.wait_send()
     for copy in x_copies:
         copy.wait_send()
@@ -407,14 +454,18 @@
         basis, coef = pl.pallas_call(
             functools.partial(kernel, n_tile),
             out_shape=(
-                jax.ShapeDtypeStruct((K * SHARE, W), F32),
-                jax.ShapeDtypeStruct((2, FR, K), F32),
+                pltpu.VMEM((K * SHARE, W), F32),
+                pltpu.VMEM((2, FR, K), F32),
             ),
             in_specs=[pl.BlockSpec(memory_space=pl.ANY)] * 4,
             out_specs=(vmem, vmem),
             scratch_shapes=[
                 pltpu.VMEM((FR, ROWS, W), BF16),
                 pltpu.VMEM((2, FR, K), BF16),
+                pltpu.VMEM((2, 4, 4 * K), BF16),
+                pltpu.VMEM((len(EARLY), SHARE, 2 * W), BF16),
+                pltpu.VMEM((ROWS, 2 * W), BF16),
+                pltpu.VMEM((len(EARLY) * SHARE, FR * W), F32),
                 pltpu.VMEM((1, 2 * RAD + 1), BF16),
                 pltpu.VMEM((1, 2 * RAD + 1), BF16),
                 pltpu.VMEM((ROWS, FR * W), F32),
@@ -423,7 +474,7 @@
                 pltpu.VMEM((2, SHARE * FR, W), F32),
                 pltpu.VMEM((N_TM, SHARE, FR, W), BF16),
                 pltpu.VMEM((SHARE, FRAMES, W), BF16),
-                pltpu.VMEM((N_TM, FR, K), BF16),
+                pltpu.VMEM((N_TM, 4, 4 * K), BF16),
                 pltpu.VMEM((HALF, K, FRAMES), BF16),
                 pltpu.VMEM((HALF, 8, 128), F32),
                 pltpu.VMEM((K, FRAMES), BF16),
@@ -435,6 +486,7 @@
                 pltpu.VMEM((3 * K, PIX), BF16),
                 pltpu.VMEM((K, PIX), F32),
                 dma((4,)), dma((2,)), dma((2,)), dma((N_TM,)), dma((N_TM,)), dma((N_TM,)), dma((N_TM,)),
+                dma((len(EARLY),)), dma((len(EARLY),)),
                 dma((HALF,)), dma((HALF,)), dma((HALF,)), dma((HALF,)),
                 dma((N_TM,)), dma((N_TM,)), dma((N_TM,)), dma((N_TM,)),
             ],
@@ -446,8 +498,7 @@
             time_taps.reshape(1, -1),
             space_taps.reshape(1, -1),
         )
-        scale = math.sqrt(ROWS // 2 * W)
-        return basis.reshape(K, SHARE, W) * scale, jnp.transpose(coef * scale, (0, 2, 1))[:, None]
+        return basis.reshape(K, SHARE, W), jnp.transpose(coef, (0, 2, 1))[:, None]
 
     in_specs = (P("tm", None, "tile"), P(None, "tile", None, "tm"), P(), P())
     out_specs = (P(None, "tm", "tile"), P(None, "tile", None, "tm"))

time: 63.6 us -> 57.6 us (0.906)
  Pallas kernels: 60.5 us -> 55.5 us
  other arithmetic: 2.28 us -> 0 us
  local copies, waits for them, and re-layouts: 0.01 us -> 1.31 us
    pallas_call x1, Pallas kernels: 60.5 us -> 55.5 us  [local(): pl.pallas_call(functools.partial(kernel, n_tile), out_shape=(pltpu.VMEM((...]
    mul x1 -> x0, other arithmetic: 1.68 us -> none  [local(): basis.reshape(K, SHARE, W) * scale]
    unnamed x2, local copies, waits for them, and re-layouts: 0.01 us -> 1.31 us
where the time goes in v3:
time: 57.6 us; the launch traced here: 57.5 us
  Pallas kernels  55.5 us (96%)
  local copies, waits for them, and re-layouts  1.31 us (2%)
  between operations  0.64 us (1%)
    pallas_call x1, Pallas kernels, local(): pl.pallas_call(functools.partial(kernel, n_tile), out_shape=(pltpu.VMEM((...  55.5 us
    unnamed x2, local copies, waits for them, and re-layouts  1.31 us

profile of v3, /device:TPU:1, one launch (start us, length us, event | category | flops | bytes accessed | tf_op | source)
XLA Modules:
  0.0 57.5 jit_solution(6397315279340608001)
XLA Ops:
  0.6 55.5 %low_rank.1 = (f32[512,128]{1,0:T(8,128)S(1)}, f32[2,16,32]{2,1,0:T(8,128)S(1)}) custom-call(bf16[16,256,128]{2,1,0:T(8,128)(2,1)} %movie_hbm.1, bf16[2,16,32]{2,1,0:T(8,128)(2,1)} %bitcast.13, bf16[1,17]{1,0:T(2,128)(2,1)} %bitcast.14, bf16[1,17]{1,0:T(2,128)(2,1)} %bitcast.15), custom_call_target="tpu_custom_call" | custom-call | tf_op jit(solution)/shard_map/low_rank/pallas_call | solution.py:454
  56.2 0.7 %copy.9 = f32[32,16,128]{2,1,0:T(8,128)} copy(f32[32,16,128]{2,1,0:T(8,128)S(1)} %bitcast.11) | data formatting | bytes 524288
  56.9 0.6 %copy.10 = f32[2,1,32,16]{2,3,1,0:T(8,128)} copy(f32[2,1,32,16]{2,3,1,0:T(8,128)S(1)} %bitcast.12) | data formatting | bytes 8192

commit v4 on v3

--- a/solution.py
+++ b/solution.py
@@ -77,8 +77,8 @@
     return out
 
 
-def gram(x3):
-    return fold_lanes(fold(mm_nt(x3, x3), 3), 3)
+def gram(x2):
+    return fold_lanes(fold(mm_nt(x2, x2), 2), 2)
 
 
 def inverse_factors(grams):
@@ -138,6 +138,10 @@
         ref[:, i * K : (i + 1) * K] = g[8 * i : 8 * i + 8, :]
 
 
+def unpack_rows(total):
+    return jnp.concatenate([total[:, i * K : (i + 1) * K] for i in range(4)], axis=0)
+
+
 def unpack_gram(total):
     return jnp.concatenate([total[:, i * K : (i + 1) * K] for i in range(4)], axis=0)
 
@@ -147,7 +151,7 @@
     movie_hbm, omega_hbm, time_hbm, space_hbm,
     basis_ref, coef_ref,
     movie, omega_ref, om_mine, fix, rim_buf, share, time_ref, space_ref, far, packed, edge, turn, out_buf, seen, om_all,
-    b_slots, g_slots, b_mine, g_mine, h_mine, h_slots, d_mine, d_slots, y_buf, r_buf,
+    b_slots, g_slots, b_mine, g_mine, orders, h_mine, h_slots, d_mine, d_slots, y_buf, r_buf,
     load_sem, halo_s, halo_r, s_s, s_r, om_s, om_r, c_s, c_r, b_s, b_r, g_s, g_r, h_s, h_r, d_s, d_r,
 ):
     tile = lax.axis_index("tile")
@@ -312,7 +316,10 @@
     om = jnp.concatenate([om[:, a * K : (a + 1) * K] for a in range(4)], axis=0).astype(BF16)
     n_id = iota((FRAMES, FRAMES), 0)
     at = lax.rem(n_id, 64) // 4 * FR + n_id // 64 * 4 + lax.rem(n_id, 4)
-    om = mm_tn(om, jnp.where(at == iota((FRAMES, FRAMES), 1), 1.0, 0.0).astype(BF16))
+    order = jnp.where(at == iota((FRAMES, FRAMES), 1), 1.0, 0.0).astype(BF16)
+    om = mm_tn(om, order)
+    orders[0] = order
+    orders[1] = mm(order, low).astype(BF16)
     probe = om - mm(om.astype(BF16), low)
     probe2 = stacked(probe, 2)
 
@@ -341,7 +348,7 @@
         return jnp.concatenate([seen[2 * i], seen[2 * i + 1]], axis=1)
 
     for i in range(SHARE // 2):
-        y_buf[:, i * 256 : (i + 1) * 256] = stacked(fold(mm(probe2, pair(i)), 2), 3)
+        y_buf[:, i * 256 : (i + 1) * 256] = stacked(fold(mm(probe2, pair(i)), 2), 2)
     pack_gram(g_mine, gram(y_buf[...]))
     x_copies = []
 
@@ -365,10 +372,10 @@
             ).wait_recv()
 
     to_half(g_mine, g_slots, g_s, g_r)
-    back = jnp.zeros((3 * K, FRAMES), F32)
+    back = jnp.zeros((2 * K, FRAMES), F32)
     for i in range(SHARE // 2):
         back = back + mm_nt(y_buf[:, i * 256 : (i + 1) * 256], pair(i))
-    b_mine[...] = fold(back, 3).astype(BF16)
+    b_mine[...] = fold(back, 2).astype(BF16)
     to_half(b_mine, b_slots, b_s, b_r)
     from_half(g_mine, g_slots, g_s, g_r)
     g_sum = g_slots[0]
@@ -386,12 +393,14 @@
     for i in range(SHARE // 2):
         r = fold(mm(probe2, pair(i)), 2)
         r_buf[:, i * 256 : (i + 1) * 256] = r
-        y_buf[:, i * 256 : (i + 1) * 256] = stacked(r, 3)
+        y_buf[:, i * 256 : (i + 1) * 256] = stacked(r, 2)
     pack_gram(h_mine, gram(y_buf[...]))
 
-    def to_all(src, dst, ss, rs):
-        for k in far_first:
-            peer = lax.rem(me + k, N_TM)
+    own_first = [half * HALF + lax.rem(place + k, HALF) for k in (4, 3, 5, 2, 6, 1, 7)]
+    own_first += [(1 - half) * HALF + lax.rem(place + k, HALF) for k in (0, 1, 7, 2, 6, 3, 5, 4)]
+
+    def to_all(peers, src, dst, ss, rs):
+        for peer in peers:
             copy = pltpu.make_async_remote_copy(
                 src_ref=src(peer), dst_ref=dst.at[me], send_sem=ss.at[peer], recv_sem=rs.at[me],
                 device_id=(tile, peer), device_id_type=MESH,
@@ -399,43 +408,50 @@
             copy.start()
             x_copies.append(copy)
 
-    def from_all(src, dst, ss, rs):
-        for k in range(1, N_TM):
-            source = lax.rem(me + k, N_TM)
+    def from_all(sources, src, dst, ss, rs):
+        for source in sources:
             pltpu.make_async_remote_copy(
                 src_ref=src(source), dst_ref=dst.at[source], send_sem=ss.at[source], recv_sem=rs.at[source],
                 device_id=(tile, source), device_id_type=MESH,
             ).wait_recv()
 
-    to_all(lambda peer: h_mine, h_slots, h_s, h_r)
+    to_all(own_first[7:] + own_first[:7], lambda peer: h_mine, h_slots, h_s, h_r)
     h_slots[me] = h_mine[...]
-    down_p = jnp.zeros((FRAMES, 2 * K), F32)
+    down_p = jnp.zeros((2 * K, FRAMES), F32)
     for i in range(SHARE // 2):
-        down_p = down_p + mm_nt(pair(i), y_buf[: 2 * K, i * 256 : (i + 1) * 256])
-    moved = fold_lanes(down_p, 2)
-    moved = moved - fold_lanes(mm(low, stacked(moved, 2, axis=1)), 2)
-    d_mine[...] = moved.astype(BF16).reshape(N_TM, FR, K)
-    to_all(lambda peer: d_mine.at[peer], d_slots, d_s, d_r)
+        down_p = down_p + mm_nt(y_buf[:, i * 256 : (i + 1) * 256], pair(i))
+    moved = stacked(fold(down_p, 2), 2)
+    moved = fold_lanes(mm_nt(orders[0], moved) - mm_nt(orders[1], moved), 2)
+    moved = jnp.concatenate([moved[64 * a : 64 * a + 64] for a in range(4)], axis=1)
+    d_mine[...] = moved.reshape(N_TM, 4, 4 * K).astype(BF16)
+    to_all([lax.rem(me + k, N_TM) for k in far_first], lambda peer: d_mine.at[peer], d_slots, d_s, d_r)
     d_slots[me] = d_mine[me]
-    from_all(lambda peer: h_mine, h_slots, h_s, h_r)
-    grams = []
-    for s in range(2):
-        total = h_slots[s * HALF]
+
+    def factor_of(side):
+        total = h_slots[side * HALF]
         for i in range(1, HALF):
-            total = total + h_slots[s * HALF + i]
-        grams.append(unpack_gram(total))
-    factors = inverse_factors(grams)
-    final = jnp.where(half == 0, factors[0], factors[1]) * math.sqrt(ROWS // 2 * W)
+            total = total + h_slots[side * HALF + i]
+        return inverse_factors([unpack_gram(total)])[0]
+
+    def coefficients(side, factor):
+        total = d_slots[side * HALF].astype(F32)
+        for i in range(1, HALF):
+            total = total + d_slots[side * HALF + i].astype(F32)
+        coef_ref[side] = mm_nt(unpack_rows(total), factor, precision=HIGHEST)
+
+    other = 1 - half
+    from_all(own_first[:7], lambda peer: h_mine, h_slots, h_s, h_r)
+    own = factor_of(half)
+    final = own * math.sqrt(ROWS // 2 * W)
     for i in range(SHARE // 2):
         two = mm(final, r_buf[:, i * 256 : (i + 1) * 256], precision=HIGHEST)
         for j in range(2):
             basis_ref[pl.ds(2 * i + j, K, stride=SHARE), :] = two[:, j * W : (j + 1) * W]
-    from_all(lambda peer: d_mine.at[peer], d_slots, d_s, d_r)
-    for s in range(2):
-        total = d_slots[s * HALF].astype(F32)
-        for i in range(1, HALF):
-            total = total + d_slots[s * HALF + i].astype(F32)
-        coef_ref[s] = mm_nt(total, factors[s], precision=HIGHEST)
+    from_all(own_first[7:], lambda peer: h_mine, h_slots, h_s, h_r)
+    distant = factor_of(other)
+    from_all(own_first, lambda peer: d_mine.at[peer], d_slots, d_s, d_r)
+    coefficients(half, own)
+    coefficients(other, distant)
 
     for copy in halo:
         copy.wait_send()
@@ -443,6 +459,14 @@
         copy.wait_send()
     for copy in x_copies:
         copy.wait_send()
+
+
+def write_out(basis, coef, basis_out, coef_out, sems):
+    copies = [pltpu.make_async_copy(basis, basis_out, sems.at[0]), pltpu.make_async_copy(coef, coef_out, sems.at[1])]
+    for copy in copies:
+        copy.start()
+    for copy in copies:
+        copy.wait()
 
 
 def solution(mesh):
@@ -479,11 +503,12 @@
                 pltpu.VMEM((HALF, 8, 128), F32),
                 pltpu.VMEM((K, FRAMES), BF16),
                 pltpu.VMEM((8, 128), F32),
+                pltpu.VMEM((2, FRAMES, FRAMES), BF16),
                 pltpu.VMEM((8, 128), F32),
                 pltpu.VMEM((N_TM, 8, 128), F32),
-                pltpu.VMEM((N_TM, FR, K), BF16),
-                pltpu.VMEM((N_TM, FR, K), BF16),
-                pltpu.VMEM((3 * K, PIX), BF16),
+                pltpu.VMEM((N_TM, 4, 4 * K), BF16),
+                pltpu.VMEM((N_TM, 4, 4 * K), BF16),
+                pltpu.VMEM((2 * K, PIX), BF16),
                 pltpu.VMEM((K, PIX), F32),
                 dma((4,)), dma((2,)), dma((2,)), dma((N_TM,)), dma((N_TM,)), dma((N_TM,)), dma((N_TM,)),
                 dma((len(EARLY),)), dma((len(EARLY),)),
@@ -498,6 +523,17 @@
             time_taps.reshape(1, -1),
             space_taps.reshape(1, -1),
         )
+        basis, coef = pl.pallas_call(
+            write_out,
+            out_shape=(
+                jax.ShapeDtypeStruct((K * SHARE, W), F32),
+                jax.ShapeDtypeStruct((2, FR, K), F32),
+            ),
+            in_specs=[pl.BlockSpec(memory_space=pltpu.VMEM)] * 2,
+            out_specs=(pl.BlockSpec(memory_space=pl.ANY),) * 2,
+            scratch_shapes=[dma((2,))],
+            name="write_out",
+        )(pltpu.with_memory_space_constraint(basis, pltpu.VMEM), pltpu.with_memory_space_constraint(coef, pltpu.VMEM))
         return basis.reshape(K, SHARE, W), jnp.transpose(coef, (0, 2, 1))[:, None]
 
     in_specs = (P("tm", None, "tile"), P(None, "tile", None, "tm"), P(), P())

time: 57.6 us -> 57 us (0.990)
  local copies, waits for them, and re-layouts: 1.31 us -> 0 us
  Pallas kernels: 55.5 us -> 56.2 us
    unnamed x2 -> x0, local copies, waits for them, and re-layouts: 1.31 us -> none
    pallas_call x0 -> x1, Pallas kernels: none -> 0.72 us  [local(): pl.pallas_call(write_out, out_shape=(jax.ShapeDtypeStruct((K * SHARE, W),...]
where the time goes in v4:
time: 57 us; the launch traced here: 56.8 us
  Pallas kernels  56.2 us (99%)
  between operations  0.64 us (1%)
    pallas_call x1, Pallas kernels, local(): pl.pallas_call(functools.partial(kernel, n_tile), out_shape=(pltpu.VMEM((...  55.5 us

profile of v4, /device:TPU:1, one launch (start us, length us, event | category | flops | bytes accessed | tf_op | source)
XLA Modules:
  0.0 56.8 jit_solution(15946832265613643257)
XLA Ops:
  0.6 55.5 %low_rank.1 = (f32[512,128]{1,0:T(8,128)S(1)}, f32[2,16,32]{2,1,0:T(8,128)S(1)}) custom-call(bf16[16,256,128]{2,1,0:T(8,128)(2,1)} %movie_hbm.1, bf16[2,16,32]{2,1,0:T(8,128)(2,1)} %bitcast.11, bf16[1,17]{1,0:T(2,128)(2,1)} %bitcast.12, bf16[1,17]{1,0:T(2,128)(2,1)} %bitcast.13), custom_call_target="tpu_custom_call" | custom-call | tf_op jit(solution)/shard_map/low_rank/pallas_call | solution.py:478
  56.1 0.7 %write_out.1 = (f32[512,128]{1,0:T(8,128)}, f32[2,16,32]{2,1,0:T(8,128)}) custom-call(f32[512,128]{1,0:T(8,128)S(1)} %get-tuple-element.6.basis, f32[2,16,32]{2,1,0:T(8,128)S(1)} %get-tuple-element.7.coef), custom_call_target="tpu_custom_call" | custom-call | tf_op jit(solution)/shard_map/write_out/pallas_call | solution.py:526

commit v5 on v4

--- a/solution.py
+++ b/solution.py
@@ -23,7 +23,7 @@
 K = 32
 RAD = 8
 PIX = SHARE * W
-EARLY = (8, 7)
+EARLY = 2
 
 
 def mm(a, b, **kw):
@@ -161,6 +161,9 @@
     left = lax.rem(tile + n_tile - 1, n_tile)
     right = lax.rem(tile + 1, n_tile)
     far_first = (8, 7, 9, 6, 10, 5, 11, 4, 12, 3, 13, 2, 14, 1, 15)
+    core = lax.rem(me, 2)
+    send_order = (8, 7 + 2 * core, 9 - 2 * core) + far_first[3:]
+    recv_order = (8, 9 - 2 * core, 7 + 2 * core) + far_first[3:]
 
     loads = [
         pltpu.make_async_copy(src, dst, load_sem.at[i])
@@ -227,15 +230,15 @@
 
     s_copies = []
 
-    def block_copy(k):
-        peer = lax.rem(me + k, N_TM)
+    def block_copy(i):
+        peer = lax.rem(me + send_order[i], N_TM)
         return pltpu.make_async_remote_copy(
-            src_ref=out_buf.at[k], dst_ref=seen.at[:, rows_at(me), :],
+            src_ref=out_buf.at[i], dst_ref=seen.at[:, rows_at(me), :],
             send_sem=s_s.at[peer], recv_sem=s_r.at[me], device_id=(tile, peer), device_id_type=MESH,
         )
 
-    for i, k in enumerate(EARLY):
-        out_buf[k] = rows_of(far[rows_at(lax.rem(me + k, N_TM)), :], i % 2).astype(BF16)
+    for i in range(EARLY):
+        out_buf[i] = rows_of(far[rows_at(lax.rem(me + send_order[i], N_TM)), :], i % 2).astype(BF16)
     loads[2].wait()
     loads[3].wait()
     for i in range(2):
@@ -251,8 +254,8 @@
         )
         copy.start()
         halo.append(copy)
-    for k in EARLY:
-        s_copies.append(block_copy(k))
+    for i in range(EARLY):
+        s_copies.append(block_copy(i))
         s_copies[-1].start()
     om_copies = []
     for k in far_first:
@@ -272,8 +275,8 @@
     rim = mm(down, jnp.concatenate([rim_right, rim_left], axis=1)).astype(BF16)
     rim_buf[...] = rim
     c_copies = []
-    for i, k in enumerate(EARLY):
-        peer = lax.rem(me + k, N_TM)
+    for i in range(EARLY):
+        peer = lax.rem(me + send_order[i], N_TM)
         copy = pltpu.make_async_remote_copy(
             src_ref=rim_buf.at[rows_at(peer), :], dst_ref=fix.at[i],
             send_sem=c_s.at[i], recv_sem=c_r.at[i], device_id=(tile, peer), device_id_type=MESH,
@@ -293,16 +296,11 @@
         window = slice(2 * g * W, 2 * (g + 1) * W)
         far[:, window] = far[:, window] - mm(rim, rim_matrix(g))
 
-    for k in far_first + (0,):
-        if k in EARLY:
-            continue
-        block = rows_of(far[rows_at(lax.rem(me + k, N_TM)), :], k % 2).astype(BF16)
-        if k == 0:
-            seen[:, rows_at(me), :] = block
-        else:
-            out_buf[k] = block
-            s_copies.append(block_copy(k))
-            s_copies[-1].start()
+    for i in range(EARLY, N_TM - 1):
+        out_buf[i] = rows_of(far[rows_at(lax.rem(me + send_order[i], N_TM)), :], i % 2).astype(BF16)
+        s_copies.append(block_copy(i))
+        s_copies[-1].start()
+    seen[:, rows_at(me), :] = rows_of(far[rows_at(me), :], 1).astype(BF16)
 
     time = time_ref[...].astype(F32)
     low = toeplitz(time, FRAMES, False)
@@ -323,26 +321,25 @@
     probe = om - mm(om.astype(BF16), low)
     probe2 = stacked(probe, 2)
 
-    def block_wait(k):
-        source = lax.rem(me + N_TM - k, N_TM)
+    def block_wait(i):
+        source = lax.rem(me + N_TM - recv_order[i], N_TM)
         pltpu.make_async_remote_copy(
-            src_ref=out_buf.at[k], dst_ref=seen.at[:, rows_at(source), :],
+            src_ref=out_buf.at[i], dst_ref=seen.at[:, rows_at(source), :],
             send_sem=s_s.at[source], recv_sem=s_r.at[source], device_id=(tile, source), device_id_type=MESH,
         ).wait_recv()
 
     for copy in c_copies:
         copy.wait_recv()
-    rims_in = fix[...].reshape(len(EARLY) * SHARE, 2 * W)
+    rims_in = fix[...].reshape(EARLY * SHARE, 2 * W)
     for g in range(FR // 2):
         share[:, 2 * g * W : 2 * (g + 1) * W] = mm(rims_in, rim_matrix(g))
-    for i, k in enumerate(EARLY):
-        block_wait(k)
-        window = rows_at(lax.rem(me + N_TM - k, N_TM))
+    for i in range(EARLY):
+        block_wait(i)
+        window = rows_at(lax.rem(me + N_TM - recv_order[i], N_TM))
         moved = rows_of(share[i * SHARE : (i + 1) * SHARE, :], i % 2)
         seen[:, window, :] = (seen[:, window, :].astype(F32) - moved).astype(BF16)
-    for k in far_first:
-        if k not in EARLY:
-            block_wait(k)
+    for i in range(EARLY, N_TM - 1):
+        block_wait(i)
 
     def pair(i):
         return jnp.concatenate([seen[2 * i], seen[2 * i + 1]], axis=1)
@@ -487,9 +484,9 @@
                 pltpu.VMEM((FR, ROWS, W), BF16),
                 pltpu.VMEM((2, FR, K), BF16),
                 pltpu.VMEM((2, 4, 4 * K), BF16),
-                pltpu.VMEM((len(EARLY), SHARE, 2 * W), BF16),
+                pltpu.VMEM((EARLY, SHARE, 2 * W), BF16),
                 pltpu.VMEM((ROWS, 2 * W), BF16),
-                pltpu.VMEM((len(EARLY) * SHARE, FR * W), F32),
+                pltpu.VMEM((EARLY * SHARE, FR * W), F32),
                 pltpu.VMEM((1, 2 * RAD + 1), BF16),
                 pltpu.VMEM((1, 2 * RAD + 1), BF16),
                 pltpu.VMEM((ROWS, FR * W), F32),
@@ -511,7 +508,7 @@
                 pltpu.VMEM((2 * K, PIX), BF16),
                 pltpu.VMEM((K, PIX), F32),
                 dma((4,)), dma((2,)), dma((2,)), dma((N_TM,)), dma((N_TM,)), dma((N_TM,)), dma((N_TM,)),
-                dma((len(EARLY),)), dma((len(EARLY),)),
+                dma((EARLY,)), dma((EARLY,)),
                 dma((HALF,)), dma((HALF,)), dma((HALF,)), dma((HALF,)),
                 dma((N_TM,)), dma((N_TM,)), dma((N_TM,)), dma((N_TM,)),
             ],

time: 57 us -> 56.8 us (level)
  no operation moved by 1% of the time
where the time goes in v5:
time: 56.8 us; the launch traced here: 56.6 us
  Pallas kernels  56 us (99%)
  between operations  0.64 us (1%)
    pallas_call x1, Pallas kernels, local(): pl.pallas_call(functools.partial(kernel, n_tile), out_shape=(pltpu.VMEM((...  55.3 us

profile of v5, /device:TPU:1, one launch (start us, length us, event | category | flops | bytes accessed | tf_op | source)
XLA Modules:
  0.0 56.6 jit_solution(13364697056986054432)
XLA Ops:
  0.6 55.3 %low_rank.1 = (f32[512,128]{1,0:T(8,128)S(1)}, f32[2,16,32]{2,1,0:T(8,128)S(1)}) custom-call(bf16[16,256,128]{2,1,0:T(8,128)(2,1)} %movie_hbm.1, bf16[2,16,32]{2,1,0:T(8,128)(2,1)} %bitcast.11, bf16[1,17]{1,0:T(2,128)(2,1)} %bitcast.12, bf16[1,17]{1,0:T(2,128)(2,1)} %bitcast.13), custom_call_target="tpu_custom_call" | custom-call | tf_op jit(solution)/shard_map/low_rank/pallas_call | solution.py:475
  55.9 0.7 %write_out.1 = (f32[512,128]{1,0:T(8,128)}, f32[2,16,32]{2,1,0:T(8,128)}) custom-call(f32[512,128]{1,0:T(8,128)S(1)} %get-tuple-element.6.basis, f32[2,16,32]{2,1,0:T(8,128)S(1)} %get-tuple-element.7.coef), custom_call_target="tpu_custom_call" | custom-call | tf_op jit(solution)/shard_map/write_out/pallas_call | solution.py:523

commit v6 on v5

--- a/solution.py
+++ b/solution.py
@@ -151,7 +151,7 @@
     movie_hbm, omega_hbm, time_hbm, space_hbm,
     basis_ref, coef_ref,
     movie, omega_ref, om_mine, fix, rim_buf, share, time_ref, space_ref, far, packed, edge, turn, out_buf, seen, om_all,
-    b_slots, g_slots, b_mine, g_mine, orders, h_mine, h_slots, d_mine, d_slots, y_buf, r_buf,
+    b_slots, g_slots, b_mine, g_mine, orders, twice, h_mine, h_slots, d_mine, d_slots, y_buf, r_buf,
     load_sem, halo_s, halo_r, s_s, s_r, om_s, om_r, c_s, c_r, b_s, b_r, g_s, g_r, h_s, h_r, d_s, d_r,
 ):
     tile = lax.axis_index("tile")
@@ -318,6 +318,9 @@
     om = mm_tn(om, order)
     orders[0] = order
     orders[1] = mm(order, low).astype(BF16)
+    both = low.astype(F32) + toeplitz(time, FRAMES, True).astype(F32) - mm_tn(low, low)
+    for i, part in enumerate(pieces(both, 2)):
+        twice[i] = part
     probe = om - mm(om.astype(BF16), low)
     probe2 = stacked(probe, 2)
 
@@ -384,9 +387,9 @@
     for i in range(1, HALF):
         b_sum = b_sum + b_slots[i].astype(F32)
 
-    back = b_sum - fold(mm_nt(stacked(b_sum, 3), low), 3)
-    loadings = mm(first, back, precision=HIGHEST).astype(BF16)
-    probe2 = stacked(loadings.astype(F32) - mm(loadings, low), 2)
+    two = stacked(b_sum, 2)
+    back = b_sum - fold(mm(two, twice[0]) + mm(two, twice[1]), 2)
+    probe2 = stacked(mm(first, back, precision=HIGHEST), 2)
     for i in range(SHARE // 2):
         r = fold(mm(probe2, pair(i)), 2)
         r_buf[:, i * 256 : (i + 1) * 256] = r
@@ -437,6 +440,8 @@
         coef_ref[side] = mm_nt(unpack_rows(total), factor, precision=HIGHEST)
 
     other = 1 - half
+    for copy in halo + om_copies + s_copies + c_copies:
+        copy.wait_send()
     from_all(own_first[:7], lambda peer: h_mine, h_slots, h_s, h_r)
     own = factor_of(half)
     final = own * math.sqrt(ROWS // 2 * W)
@@ -450,10 +455,6 @@
     coefficients(half, own)
     coefficients(other, distant)
 
-    for copy in halo:
-        copy.wait_send()
-    for copy in om_copies + s_copies + c_copies:
-        copy.wait_send()
     for copy in x_copies:
         copy.wait_send()
 
@@ -501,6 +502,7 @@
                 pltpu.VMEM((K, FRAMES), BF16),
                 pltpu.VMEM((8, 128), F32),
                 pltpu.VMEM((2, FRAMES, FRAMES), BF16),
+                pltpu.VMEM((2, FRAMES, FRAMES), BF16),
                 pltpu.VMEM((8, 128), F32),
                 pltpu.VMEM((N_TM, 8, 128), F32),
                 pltpu.VMEM((N_TM, 4, 4 * K), BF16),

time: 56.8 us -> 56.6 us (level)
  no operation moved by 1% of the time
where the time goes in v6:
time: 56.6 us; the launch traced here: 56.5 us
  Pallas kernels  55.8 us (99%)
  between operations  0.64 us (1%)
    pallas_call x1, Pallas kernels, local(): pl.pallas_call(functools.partial(kernel, n_tile), out_shape=(pltpu.VMEM((...  55.1 us

profile of v6, /device:TPU:1, one launch (start us, length us, event | category | flops | bytes accessed | tf_op | source)
XLA Modules:
  0.0 56.5 jit_solution(6724638152079192450)
XLA Ops:
  0.6 55.1 %low_rank.1 = (f32[512,128]{1,0:T(8,128)S(1)}, f32[2,16,32]{2,1,0:T(8,128)S(1)}) custom-call(bf16[16,256,128]{2,1,0:T(8,128)(2,1)} %movie_hbm.1, bf16[2,16,32]{2,1,0:T(8,128)(2,1)} %bitcast.11, bf16[1,17]{1,0:T(2,128)(2,1)} %bitcast.12, bf16[1,17]{1,0:T(2,128)(2,1)} %bitcast.13), custom_call_target="tpu_custom_call" | custom-call | tf_op jit(solution)/shard_map/low_rank/pallas_call | solution.py:476
  55.7 0.7 %write_out.1 = (f32[512,128]{1,0:T(8,128)}, f32[2,16,32]{2,1,0:T(8,128)}) custom-call(f32[512,128]{1,0:T(8,128)S(1)} %get-tuple-element.6.basis, f32[2,16,32]{2,1,0:T(8,128)S(1)} %get-tuple-element.7.coef), custom_call_target="tpu_custom_call" | custom-call | tf_op jit(solution)/shard_map/write_out/pallas_call | solution.py:525

commit v7 on v6

--- a/solution.py
+++ b/solution.py
@@ -151,8 +151,8 @@
     movie_hbm, omega_hbm, time_hbm, space_hbm,
     basis_ref, coef_ref,
     movie, omega_ref, om_mine, fix, rim_buf, share, time_ref, space_ref, far, packed, edge, turn, out_buf, seen, om_all,
-    b_slots, g_slots, b_mine, g_mine, orders, twice, h_mine, h_slots, d_mine, d_slots, y_buf, r_buf,
-    load_sem, halo_s, halo_r, s_s, s_r, om_s, om_r, c_s, c_r, b_s, b_r, g_s, g_r, h_s, h_r, d_s, d_r,
+    b_slots, g_slots, b_mine, b_half, b_swap, g_mine, orders, twice, h_mine, h_slots, d_mine, d_slots, y_buf, r_buf,
+    load_sem, halo_s, halo_r, s_s, s_r, om_s, om_r, c_s, c_r, w_s, w_r, b_s, b_r, g_s, g_r, h_s, h_r, d_s, d_r,
 ):
     tile = lax.axis_index("tile")
     me = lax.axis_index("tm")
@@ -353,11 +353,10 @@
     x_copies = []
 
     def to_half(src, dst, ss, rs):
-        dst[place] = src[...]
         for k in (4, 3, 5, 2, 6, 1, 7):
             other = lax.rem(place + k, HALF)
             copy = pltpu.make_async_remote_copy(
-                src_ref=src, dst_ref=dst.at[place], send_sem=ss.at[other], recv_sem=rs.at[place],
+                src_ref=src(other), dst_ref=dst.at[place], send_sem=ss.at[other], recv_sem=rs.at[place],
                 device_id=(tile, half * HALF + other), device_id_type=MESH,
             )
             copy.start()
@@ -367,25 +366,43 @@
         for k in range(1, HALF):
             other = lax.rem(place + k, HALF)
             pltpu.make_async_remote_copy(
-                src_ref=src, dst_ref=dst.at[other], send_sem=ss.at[other], recv_sem=rs.at[other],
+                src_ref=src(other), dst_ref=dst.at[other], send_sem=ss.at[other], recv_sem=rs.at[other],
                 device_id=(tile, half * HALF + other), device_id_type=MESH,
             ).wait_recv()
 
-    to_half(g_mine, g_slots, g_s, g_r)
+    to_half(lambda other: g_mine, g_slots, g_s, g_r)
+    g_slots[place] = g_mine[...]
     back = jnp.zeros((2 * K, FRAMES), F32)
     for i in range(SHARE // 2):
         back = back + mm_nt(y_buf[:, i * 256 : (i + 1) * 256], pair(i))
-    b_mine[...] = fold(back, 2).astype(BF16)
-    to_half(b_mine, b_slots, b_s, b_r)
-    from_half(g_mine, g_slots, g_s, g_r)
+    back = fold(back, 2).astype(BF16)
+    for i in range(2):
+        b_mine[i] = back[:, i * W : (i + 1) * W]
+
+    def half_for(other):
+        return b_mine.at[lax.rem(other, 2)]
+
+    to_half(half_for, b_slots, b_s, b_r)
+    b_slots[place] = b_mine[core]
+    from_half(lambda other: g_mine, g_slots, g_s, g_r)
     g_sum = g_slots[0]
     for i in range(1, HALF):
         g_sum = g_sum + g_slots[i]
     first = inverse_factors([unpack_gram(g_sum)])[0]
-    from_half(b_mine, b_slots, b_s, b_r)
+    from_half(half_for, b_slots, b_s, b_r)
     b_sum = b_slots[0].astype(F32)
     for i in range(1, HALF):
         b_sum = b_sum + b_slots[i].astype(F32)
+    b_half[...] = b_sum
+    swap = pltpu.make_async_remote_copy(
+        src_ref=b_half, dst_ref=b_swap, send_sem=w_s, recv_sem=w_r,
+        device_id=(tile, me + 1 - 2 * core), device_id_type=MESH,
+    )
+    swap.start()
+    swap.wait_recv()
+    x_copies.append(swap)
+    given = b_swap[...]
+    b_sum = jnp.where(core == 0, jnp.concatenate([b_sum, given], axis=1), jnp.concatenate([given, b_sum], axis=1))
 
     two = stacked(b_sum, 2)
     back = b_sum - fold(mm(two, twice[0]) + mm(two, twice[1]), 2)
@@ -497,9 +514,11 @@
                 pltpu.VMEM((N_TM, SHARE, FR, W), BF16),
                 pltpu.VMEM((SHARE, FRAMES, W), BF16),
                 pltpu.VMEM((N_TM, 4, 4 * K), BF16),
-                pltpu.VMEM((HALF, K, FRAMES), BF16),
+                pltpu.VMEM((HALF, K, W), BF16),
                 pltpu.VMEM((HALF, 8, 128), F32),
-                pltpu.VMEM((K, FRAMES), BF16),
+                pltpu.VMEM((2, K, W), BF16),
+                pltpu.VMEM((K, W), F32),
+                pltpu.VMEM((K, W), F32),
                 pltpu.VMEM((8, 128), F32),
                 pltpu.VMEM((2, FRAMES, FRAMES), BF16),
                 pltpu.VMEM((2, FRAMES, FRAMES), BF16),
@@ -510,7 +529,7 @@
                 pltpu.VMEM((2 * K, PIX), BF16),
                 pltpu.VMEM((K, PIX), F32),
                 dma((4,)), dma((2,)), dma((2,)), dma((N_TM,)), dma((N_TM,)), dma((N_TM,)), dma((N_TM,)),
-                dma((EARLY,)), dma((EARLY,)),
+                dma((EARLY,)), dma((EARLY,)), dma(()), dma(()),
                 dma((HALF,)), dma((HALF,)), dma((HALF,)), dma((HALF,)),
                 dma((N_TM,)), dma((N_TM,)), dma((N_TM,)), dma((N_TM,)),
             ],

time: 56.6 us -> 57.1 us (level)
  Pallas kernels: 55.8 us -> 56.4 us
where the time goes in v7:
time: 57.1 us; the launch traced here: 57 us
  Pallas kernels  56.4 us (99%)
  between operations  0.64 us (1%)
    pallas_call x1, Pallas kernels, local(): pl.pallas_call(functools.partial(kernel, n_tile), out_shape=(pltpu.VMEM((...  55.6 us

profile of v7, /device:TPU:1, one launch (start us, length us, event | category | flops | bytes accessed | tf_op | source)
XLA Modules:
  0.0 57.0 jit_solution(1697644881791828945)
XLA Ops:
  0.6 55.6 %low_rank.1 = (f32[512,128]{1,0:T(8,128)S(1)}, f32[2,16,32]{2,1,0:T(8,128)S(1)}) custom-call(bf16[16,256,128]{2,1,0:T(8,128)(2,1)} %movie_hbm.1, bf16[2,16,32]{2,1,0:T(8,128)(2,1)} %bitcast.11, bf16[1,17]{1,0:T(2,128)(2,1)} %bitcast.12, bf16[1,17]{1,0:T(2,128)(2,1)} %bitcast.13), custom_call_target="tpu_custom_call" | custom-call | tf_op jit(solution)/shard_map/low_rank/pallas_call | solution.py:493
  56.3 0.7 %write_out.1 = (f32[512,128]{1,0:T(8,128)}, f32[2,16,32]{2,1,0:T(8,128)}) custom-call(f32[512,128]{1,0:T(8,128)S(1)} %get-tuple-element.6.basis, f32[2,16,32]{2,1,0:T(8,128)S(1)} %get-tuple-element.7.coef), custom_call_target="tpu_custom_call" | custom-call | tf_op jit(solution)/shard_map/write_out/pallas_call | solution.py:544
